TPU v7x, 768 devices: a whole 4x8x12 slice. The times are simulated.
768 devices in a mesh: dp: 24 (over z, core), tensor: 8 (over y), pipe: 4 (over x).
Axes of the slice: x: 4, y: 8, z: 12, core: 2. Of those that a mesh axis runs over, the one named last changes fastest.
Arguments:
- normed: bfloat16 [4, 10752, 16384], P('pipe', 'dp', 'tensor'), may hold values from -0.625 to 0.625
- w_value: bfloat16 [4, 16384, 1024], P('pipe', 'tensor'), may hold values from -0.5 to 0.5
- grad_value: bfloat16 [4, 10752, 1024], P('pipe', 'dp'), may hold values from -655360 to 655360
- assistant_mask: int32 [24, 4, 8192], P('dp'), may hold values from 0 to 1, as said below
Outputs:
- value_weight_grad: float32 [4, 8, 2064, 1024], P('pipe', 'tensor', 'dp')
- passed_grad: bfloat16 [4, 10752, 16384], P('pipe', 'dp', 'tensor')
Inputs may be any that keep to these rules, and one draw needn't show every extreme that they name: `assistant_mask`: assistant tokens come in runs of whole turns; every packed sequence holds at least one assistant token.
All inputs are finite; a program needn't handle non-finite values.
Results may differ from a plain program's by a relative error of at most 0.015.
Values may be sent and summed in bfloat16 or wider, within the bound.
No kernel may reach another device: no remote copies, remote signals or barrier semaphores. Data moves between devices by JAX's collectives and lax.ppermute only.
A program may use at most 64 MiB of HBM per device.

v0:
```python
import jax
import jax.numpy as jnp
from jax import lax
from jax.sharding import PartitionSpec as P

HEAD = 128
KV_HEADS = 8


def from_behind(block, axis, distance):
    devices = range(lax.axis_size(axis))
    route = [(i - distance, i) for i in devices if i - distance in devices]
    return lax.ppermute(block, axis, route)


def local(normed, w_value, grad_value, assistant_mask):
    local_count = jnp.sum(assistant_mask, dtype=jnp.int32)
    mask_total = lax.psum(local_count, "dp")
    divisor = mask_total.astype(jnp.float32)
    inputs = normed[0]
    weight = w_value[0]
    upstream = grad_value[0]
    local_width = inputs.shape[1]
    replicas = lax.axis_size("dp")
    padded_rows = (local_width + replicas - 1) // replicas * replicas
    padded = jnp.pad(inputs, ((0, 0), (0, padded_rows - local_width)))
    weight_sum = lax.psum_scatter(
        lax.dot_general(
            padded, upstream, (((0,), (0,)), ((), ())), preferred_element_type=jnp.float32
        ).astype(jnp.bfloat16),
        "dp",
        scatter_dimension=0,
        tiled=True,
    ).astype(jnp.float32)
    total = jnp.zeros((upstream.shape[0], local_width), jnp.float32)
    for head in range(KV_HEADS):
        piece_up = upstream[:, head * HEAD : (head + 1) * HEAD]
        piece_w = weight[:, head * HEAD : (head + 1) * HEAD]
        part = lax.dot_general(
            piece_up, piece_w, (((1,), (1,)), ((), ())), preferred_element_type=jnp.float32
        ).astype(jnp.bfloat16)
        total = total + part.astype(jnp.float32)
    weight_grad = weight_sum / divisor
    input_grad = (total / divisor).astype(jnp.bfloat16)
    passed = from_behind(input_grad, "pipe", -1)
    return (weight_grad[None, None], passed[None])


def solution(mesh):
    return jax.shard_map(
        local,
        mesh=mesh,
        in_specs=(
            P("pipe", "dp", "tensor"),
            P("pipe", "tensor", None),
            P("pipe", "dp", None),
            P("dp", None, None),
        ),
        out_specs=(P("pipe", "tensor", "dp", None), P("pipe", "dp", "tensor")),
        check_vma=False,
    )
```

profile of v0, /device:TPU:1, one launch (start us, length us, event | category | flops | bytes accessed | tf_op | source)
XLA Modules:
  0.0 131.3 jit_solution(16533108662788245180)
XLA Ops:
  0.6 0.0 copy-start
  0.6 0.0 copy-start.1
  0.7 1.9 %convolution_convert_fusion.1 = bf16[448,2048]{1,0:T(8,128)(2,1)S(1)} fusion(bf16[2048,1024]{1,0:T(8,128)(2,1)} %bitcast.11, bf16[448,1024]{1,0:T(8,128)(2,1)} %bitcast.20), kind=kOutput, calls=%fused_computation.2 | convolution fusion | flops 235798528 | bytes 2473984 | tf_op jit(solution)/shard_map/dot_general | solution.py:39
  2.6 3.0 %convolution_convert_fusion.2 = bf16[448,2048]{1,0:T(8,128)(2,1)} fusion(bf16[2048,1024]{1,0:T(8,128)(2,1)} %bitcast.12, bf16[448,1024]{1,0:T(8,128)(2,1)} %bitcast.21), kind=kOutput, calls=%fused_computation.3 | convolution fusion | flops 235798528 | bytes 2473984 | tf_op jit(solution)/shard_map/dot_general | solution.py:39
  5.5 2.8 %convolution_convert_fusion.3 = bf16[448,2048]{1,0:T(8,128)(2,1)} fusion(bf16[2048,1024]{1,0:T(8,128)(2,1)S(1)} %bitcast.15, bf16[448,1024]{1,0:T(8,128)(2,1)} %bitcast.22), kind=kOutput, calls=%fused_computation.4 | convolution fusion | flops 235798528 | bytes 2473984 | tf_op jit(solution)/shard_map/dot_general | solution.py:39
  8.3 1.9 %convolution_convert_fusion.4 = bf16[448,2048]{1,0:T(8,128)(2,1)} fusion(bf16[2048,1024]{1,0:T(8,128)(2,1)S(1)} %bitcast.16, bf16[448,1024]{1,0:T(8,128)(2,1)S(1)} %bitcast.23), kind=kOutput, calls=%fused_computation.5 | convolution fusion | flops 235798528 | bytes 2473984 | tf_op jit(solution)/shard_map/dot_general | solution.py:39
  10.2 1.9 %convolution_convert_fusion.5 = bf16[448,2048]{1,0:T(8,128)(2,1)} fusion(bf16[2048,1024]{1,0:T(8,128)(2,1)S(1)} %bitcast.17, bf16[448,1024]{1,0:T(8,128)(2,1)S(1)} %bitcast.24), kind=kOutput, calls=%fused_computation.6 | convolution fusion | flops 235798528 | bytes 2473984 | tf_op jit(solution)/shard_map/dot_general | solution.py:39
  12.1 1.9 %convolution_convert_fusion.6 = bf16[448,2048]{1,0:T(8,128)(2,1)} fusion(bf16[2048,1024]{1,0:T(8,128)(2,1)S(1)} %bitcast.18, bf16[448,1024]{1,0:T(8,128)(2,1)S(1)} %bitcast.25), kind=kOutput, calls=%fused_computation.7 | convolution fusion | flops 235798528 | bytes 2473984 | tf_op jit(solution)/shard_map/dot_general | solution.py:39
  14.1 0.7 reduce_sum.9
  14.8 3.0 %convolution_convert_fusion.7 = bf16[448,2048]{1,0:T(8,128)(2,1)} fusion(bf16[2048,1024]{1,0:T(8,128)(2,1)} %bitcast.13, bf16[448,1024]{1,0:T(8,128)(2,1)S(1)} %bitcast.26), kind=kOutput, calls=%fused_computation.8 | convolution fusion | flops 235798528 | bytes 2473984 | tf_op jit(solution)/shard_map/dot_general | solution.py:39
  17.8 46.0 %psum.7 = s32[]{:T(128)} all-reduce(s32[]{:T(128)} %reduce_sum.9), channel_id=1, replica_groups=mesh['dp'=24,'tensor'=8,'pipe'=4] {'dp'}, use_global_device_ids=true, to_apply=%region_2.3 | all-reduce | flops 1 | bytes 8 | tf_op jit(solution)/shard_map/psum | solution.py:18
  64.4 0.0 copy-start.3
  64.4 7.8 %divide_convert_fusion = bf16[448,2048]{1,0:T(8,128)(2,1)} fusion(bf16[448,2048]{1,0:T(8,128)(2,1)S(1)} %convolution_convert_fusion.1, bf16[448,2048]{1,0:T(8,128)(2,1)} %convolution_convert_fusion.2, bf16[448,2048]{1,0:T(8,128)(2,1)} %convolution_convert_fusion.3, bf16[448,2048]{1,0:T(8,128)(2,1)} %convolution_convert_fusion.4, ...), kind=kOutput, calls=%fused_computation.1 | convolution fusion | flops 251396096 | bytes 15319044 | tf_op jit(solution)/shard_map/dot_general | solution.py:39
  72.2 1.3 collective-permute-start
  73.5 4.4 %convolution_convert_fusion = bf16[2064,1024]{1,0:T(8,128)(2,1)} fusion(bf16[448,2048]{1,0:T(8,128)(2,1)S(1)} %bitcast.28, bf16[1,448,1024]{2,1,0:T(8,128)(2,1)S(1)} %copy-done.1), kind=kOutput, calls=%fused_computation | convolution fusion | flops 1895841792 | bytes 6979584 | tf_op jit(solution)/shard_map/dot_general | solution.py:28
  77.9 46.8 %fusion = bf16[88,1024]{1,0:T(8,128)(2,1)S(1)} fusion(bf16[2064,1024]{1,0:T(8,128)(2,1)} %convolution_convert_fusion), kind=kCustom, calls=%all-reduce-scatter | all-reduce-scatter fusion | flops 2162689 | bytes 4411392
  124.7 1.9 %collective-permute-start.1 = (bf16[46,1024]{1,0:T(8,128)(2,1)S(1)}, bf16[46,1024]{1,0:T(8,128)(2,1)S(1)}, u32[]{:S(2)}, u32[]{:S(2)}) collective-permute-start(bf16[46,1024]{1,0:T(8,128)(2,1)S(1)} %slice.80), channel_id=1, source_target_pairs={{0,32},{32,64},{64,96},{96,128},{128,160},{160,192},{192,224},{224... | collective-permute-start | bytes 282632
  126.7 1.3 dynamic-slice.4
  128.6 0.0 collective-permute-done.1
  128.6 0.3 concatenate
  128.9 0.1 divide_bitcast_fusion
  129.0 1.1 copy.7
  130.1 0.0 collective-permute-done
  130.1 1.2 copy.9
  (6 shorter events, 0.0 us)
Async XLA Ops:
  0.6 4.9 %copy-start = (bf16[1,2048,1024]{2,1,0:T(8,128)(2,1)S(1)}, bf16[1,2048,1024]{2,1,0:T(8,128)(2,1)}, u32[]{:S(2)}) copy-start(bf16[1,2048,1024]{2,1,0:T(8,128)(2,1)} %param.5) | copy-start | bytes 12582916
  0.6 7.7 %copy-start.1 = (bf16[1,448,1024]{2,1,0:T(8,128)(2,1)S(1)}, bf16[1,448,1024]{2,1,0:T(8,128)(2,1)}, u32[]{:S(2)}) copy-start(bf16[1,448,1024]{2,1,0:T(8,128)(2,1)} %param.6) | copy-start | bytes 2752516
  8.3 5.7 %copy-start.2 = (s32[1,4,8192]{2,1,0:T(4,128)S(1)}, s32[1,4,8192]{2,1,0:T(4,128)}, u32[]{:S(2)}) copy-start(s32[1,4,8192]{2,1,0:T(4,128)} %param.7) | copy-start | bytes 393220
  64.4 9.1 %copy-start.3 = (bf16[1,448,2048]{2,1,0:T(8,128)(2,1)S(1)}, bf16[1,448,2048]{2,1,0:T(8,128)(2,1)}, u32[]{:S(2)}) copy-start(bf16[1,448,2048]{2,1,0:T(8,128)(2,1)} %param.4) | copy-start | bytes 5505028
  72.2 57.8 %collective-permute-start = (bf16[448,2048]{1,0:T(8,128)(2,1)}, bf16[448,2048]{1,0:T(8,128)(2,1)S(1)}, u32[]{:S(2)}, u32[]{:S(2)}) collective-permute-start(bf16[448,2048]{1,0:T(8,128)(2,1)} %divide_convert_fusion), channel_id=1, source_target_pairs={{1,0},{2,1},{3,2},{5,4},{6,5},{7,6},{9,8},{10,9},{11,10},{13,12},{... | collective-permute-start | bytes 5505032 | tf_op jit(solution)/shard_map/ppermute | solution.py:13
  124.7 3.9 %collective-permute-start.1 = (bf16[46,1024]{1,0:T(8,128)(2,1)S(1)}, bf16[46,1024]{1,0:T(8,128)(2,1)S(1)}, u32[]{:S(2)}, u32[]{:S(2)}) collective-permute-start(bf16[46,1024]{1,0:T(8,128)(2,1)S(1)} %slice.80), channel_id=1, source_target_pairs={{0,32},{32,64},{64,96},{96,128},{128,160},{160,192},{192,224},{224... | collective-permute-start | bytes 282632
where the time goes:
time: 132 us; the launch traced here: 131 us
  blocking collectives  92.8 us (70%)
  matrix products  28.6 us (22%)
  local copies, waits for them, and re-layouts  3.93 us (3%)
  starting transfers between devices  3.2 us (2%)
  between operations  2.04 us (2%)
    unnamed x1, blocking collectives  46.8 us
    psum x1, blocking collectives, local(): mask_total = lax.psum(local_count, 'dp')  46 us
    dot_general x8, matrix products, local(): lax.dot_general(piece_up, piece_w, (((1,), (1,)), ((), ())), preferred_el...  24.2 us
    dot_general x1, matrix products, local(): lax.dot_general(padded, upstream, (((0,), (0,)), ((), ())), preferred_ele...  4.36 us
    unnamed x13, local copies, waits for them, and re-layouts  3.93 us
  transfers between devices with their start and end apart: 2, of which 0 were waited for; matrix products, arithmetic and copies ran while one was open for 41% of the time, Pallas kernels for 0%

commit v1 on v0

v1 whole, which is shorter than its diff:
```python
import functools

import jax
import jax.numpy as jnp
from jax import lax
from jax.experimental import pallas as pl
from jax.experimental.pallas import tpu as pltpu
from jax.sharding import PartitionSpec as P

DIGITS = 6


def from_behind(block, axis, distance):
    devices = range(lax.axis_size(axis))
    route = [(i - distance, i) for i in devices if i - distance in devices]
    return lax.ppermute(block, axis, route)


def term_kernel(n, rows, mask_ref, normed_ref, grad_ref, out_ref, spread_ref):
    tokens, width = normed_ref.shape
    pieces = []
    for d in range(n):
        low, high = d * rows, min((d + 1) * rows, width)
        pieces += [normed_ref[:, low:high], jnp.zeros((tokens, rows + 1 - (high - low)), jnp.bfloat16)]
    spread_ref[...] = jnp.concatenate(pieces, axis=1)
    count = jnp.sum(mask_ref[...])
    lane = lax.broadcasted_iota(jnp.int32, (1, out_ref.shape[1]), 1)
    digit = jnp.bitwise_and(jnp.right_shift(count, 3 * jnp.minimum(lane, DIGITS)), 7).astype(jnp.float32)
    digit = jnp.where(lane < DIGITS, digit, 0.0)
    step = 256
    for m in range(0, out_ref.shape[0], step):
        size = min(step, out_ref.shape[0] - m)
        tile = lax.dot_general(
            spread_ref[:, m : m + size], grad_ref[...], (((0,), (0,)), ((), ())), preferred_element_type=jnp.float32
        )
        row = lax.broadcasted_iota(jnp.int32, (size, 1), 0) + (m + 1)
        out_ref[m : m + size, :] = jnp.where(row % (rows + 1) == 0, digit, tile).astype(jnp.bfloat16)


def terms(inputs, upstream, mask, n, rows):
    total = n * (rows + 1)
    return pl.pallas_call(
        functools.partial(term_kernel, n, rows),
        out_shape=jax.ShapeDtypeStruct((total, upstream.shape[1]), jnp.bfloat16),
        in_specs=[pl.BlockSpec(memory_space=pltpu.VMEM)] * 3,
        out_specs=pl.BlockSpec(memory_space=pltpu.VMEM),
        scratch_shapes=[pltpu.VMEM((inputs.shape[0], total), jnp.bfloat16)],
        name="terms",
        cost_estimate=pl.CostEstimate(flops=2 * inputs.size * upstream.shape[1], bytes_accessed=8 << 20, transcendentals=0),
    )(mask, inputs, upstream)


def local(normed, w_value, grad_value, assistant_mask):
    inputs = normed[0]
    weight = w_value[0]
    upstream = grad_value[0]
    n = lax.axis_size("dp")
    rows = -(-inputs.shape[1] // n)

    total = lax.dot_general(upstream, weight, (((1,), (1,)), ((), ())), preferred_element_type=jnp.float32).astype(jnp.bfloat16)
    passed = from_behind(total, "pipe", -1)
    upstream, inputs, _ = lax.optimization_barrier((upstream, inputs, total))
    mask = assistant_mask.reshape(-1, 128)
    term = terms(inputs, upstream, mask, n, rows)
    mine = lax.psum_scatter(term, "dp", scatter_dimension=0, tiled=True).astype(jnp.float32)
    scale = 8 ** jnp.arange(DIGITS, dtype=jnp.int32)
    divisor = jnp.sum(mine[rows, :DIGITS] * scale.astype(jnp.float32))
    weight_grad = mine[:rows] / divisor
    input_grad = (passed.astype(jnp.float32) / divisor).astype(jnp.bfloat16)
    return (weight_grad[None, None], input_grad[None])


def solution(mesh):
    return jax.shard_map(
        local,
        mesh=mesh,
        in_specs=(
            P("pipe", "dp", "tensor"),
            P("pipe", "tensor", None),
            P("pipe", "dp", None),
            P("dp", None, None),
        ),
        out_specs=(P("pipe", "tensor", "dp", None), P("pipe", "dp", "tensor")),
        check_vma=False,
    )
```

time: 132 us -> 83.2 us (0.63)
  blocking collectives: 92.8 us -> 55.2 us
  matrix products: 28.6 us -> 5.83 us
  Pallas kernels: 0 us -> 7.46 us
  other arithmetic: 0.76 us -> 3.78 us
    psum x1 -> x0, blocking collectives: 46 us -> none  [local(): mask_total = lax.psum(local_count, 'dp')]
    dot_general x9 -> x1, matrix products: 28.6 us -> 5.83 us  [local(): lax.dot_general(upstream, weight, (((1,), (1,)), ((), ())), preferred_ele...]
    unnamed x1, blocking collectives: 46.8 us -> 55.2 us
    pallas_call x0 -> x1, Pallas kernels: none -> 7.46 us  [terms(): pl.pallas_call(functools.partial(term_kernel, n, rows), out_shape=jax.Sha...]
    broadcast_in_dim x1 -> x2, other arithmetic: 0.06 us -> 3.05 us  [local(): return (weight_grad[None, None], input_grad[None])]
    unnamed x13 -> x6, local copies, waits for them, and re-layouts: 3.93 us -> 2.64 us
  transfers between devices with their start and end apart: 2 -> 2, of which waited for: 0 -> 1; matrix products, arithmetic and copies ran while one was open for 41% -> 73% of each run, Pallas kernels for 0% -> 9%
where the time goes in v1:
time: 83.2 us; the launch traced here: 81.9 us
  blocking collectives  55.2 us (66%)
  Pallas kernels  7.46 us (9%)
  matrix products  5.83 us (7%)
  starting transfers between devices  4.31 us (5%)
  other arithmetic  3.78 us (5%)
  local copies, waits for them, and re-layouts  3.38 us (4%)
  between operations  1.36 us (2%)
    unnamed x1, blocking collectives  55.2 us
    pallas_call x1, Pallas kernels, terms(): pl.pallas_call(functools.partial(term_kernel, n, rows), out_shape=jax.Sha...  7.46 us
    dot_general x1, matrix products, local(): lax.dot_general(upstream, weight, (((1,), (1,)), ((), ())), preferred_ele...  5.83 us
    broadcast_in_dim x2, other arithmetic, local(): return (weight_grad[None, None], input_grad[None])  3.05 us
    unnamed x1, starting transfers between devices  3.03 us
    unnamed x6, local copies, waits for them, and re-layouts  2.64 us
  transfers between devices with their start and end apart: 2, of which 1 were waited for; matrix products, arithmetic and copies ran while one was open for 73% of the time, Pallas kernels for 9%

profile of v1, /device:TPU:1, one launch (start us, length us, event | category | flops | bytes accessed | tf_op | source)
XLA Modules:
  0.0 81.9 jit_solution(5300844690755191817)
XLA Ops:
  0.6 0.0 copy-start
  0.6 5.8 %fusion.3 = bf16[448,2048]{1,0:T(8,128)(2,1)} fusion(bf16[1,2048,1024]{2,1,0:T(8,128)(2,1)} %param.5, bf16[1,448,1024]{2,1,0:T(8,128)(2,1)} %param.6), kind=kOutput, calls=%fused_computation.3 | convolution fusion | flops 1879965696 | bytes 6946816 | tf_op jit(solution)/shard_map/dot_general | solution.py:60
  6.5 1.3 %collective-permute-start = (bf16[448,2048]{1,0:T(8,128)(2,1)}, bf16[448,2048]{1,0:T(8,128)(2,1)S(1)}, u32[]{:S(2)}, u32[]{:S(2)}) collective-permute-start(bf16[448,2048]{1,0:T(8,128)(2,1)} %fusion.3), channel_id=1, source_target_pairs={{1,0},{2,1},{3,2},{5,4},{6,5},{7,6},{9,8},{10,9},{11,10},{13,12},{... | collective-permute-start | bytes 5505032 | tf_op jit(solution)/shard_map/ppermute | solution.py:16
  7.8 0.0 copy-done
  7.8 0.7 reshape.7.mask_ref
  8.5 7.5 %terms.1 = bf16[2088,1024]{1,0:T(8,128)(2,1)} custom-call(s32[256,128]{1,0:T(8,128)} %reshape.7.mask_ref, bf16[448,2048]{1,0:T(8,128)(2,1)} %bitcast.22, bf16[448,1024]{1,0:T(8,128)(2,1)} %bitcast.23), custom_call_target="tpu_custom_call" | custom-call | flops 1879048192 | bytes 8388608 | tf_op jit(solution)/shard_map/terms/pallas_call | solution.py:42
  16.0 55.2 %fusion = bf16[88,1024]{1,0:T(8,128)(2,1)S(1)} fusion(bf16[2088,1024]{1,0:T(8,128)(2,1)} %terms.1), kind=kCustom, calls=%all-reduce-scatter | all-reduce-scatter fusion | flops 2162689 | bytes 4460544
  71.2 3.0 %collective-permute-start.1 = (bf16[23,1024]{1,0:T(8,128)(2,1)S(1)}, bf16[23,1024]{1,0:T(8,128)(2,1)S(1)}, u32[]{:S(2)}, u32[]{:S(2)}) collective-permute-start(bf16[23,1024]{1,0:T(8,128)(2,1)S(1)} %slice.10), channel_id=1, source_target_pairs={{0,32},{32,64},{64,96},{96,128},{128,160},{160,192},{192,224},{224... | collective-permute-start | bytes 141320
  74.2 1.3 %dynamic-slice.4 = u32[1]{0:T(128)} dynamic-slice(u32[768]{0:T(1024)} %constant.30, u32[]{:S(6)} %partition-id.4), dynamic_slice_sizes={1} | dynamic-slice | bytes 12
  76.2 0.6 collective-permute-done.1
  76.7 0.2 concatenate
  77.0 0.7 fusion.12
  77.7 0.7 fusion.7
  78.5 1.1 %copy.7 = f32[1,1,86,1024]{3,1,2,0:T(1,128)} copy(f32[1,1,86,1024]{3,2,1,0:T(8,128)S(1)} %fusion.7) | data formatting | bytes 704512
  79.6 0.0 collective-permute-done
  79.6 2.3 %fusion.6 = bf16[1,448,2048]{2,1,0:T(8,128)(2,1)} fusion(bf16[448,2048]{1,0:T(8,128)(2,1)S(1)} %collective-permute-done, f32[]{:T(128)} %fusion.12), kind=kLoop, calls=%fused_computation.4 | loop fusion | flops 2752512 | bytes 3670020 | tf_op jit(solution)/shard_map/broadcast_in_dim | solution.py:70
  (2 shorter events, 0.1 us)
Async XLA Ops:
  0.6 7.1 %copy-start = (s32[1,4,8192]{2,1,0:T(4,128)S(1)}, s32[1,4,8192]{2,1,0:T(4,128)}, u32[]{:S(2)}) copy-start(s32[1,4,8192]{2,1,0:T(4,128)} %param.7) | copy-start | bytes 393220
  6.5 73.1 %collective-permute-start = (bf16[448,2048]{1,0:T(8,128)(2,1)}, bf16[448,2048]{1,0:T(8,128)(2,1)S(1)}, u32[]{:S(2)}, u32[]{:S(2)}) collective-permute-start(bf16[448,2048]{1,0:T(8,128)(2,1)} %fusion.3), channel_id=1, source_target_pairs={{1,0},{2,1},{3,2},{5,4},{6,5},{7,6},{9,8},{10,9},{11,10},{13,12},{... | collective-permute-start | bytes 5505032 | tf_op jit(solution)/shard_map/ppermute | solution.py:16
  71.2 5.5 %collective-permute-start.1 = (bf16[23,1024]{1,0:T(8,128)(2,1)S(1)}, bf16[23,1024]{1,0:T(8,128)(2,1)S(1)}, u32[]{:S(2)}, u32[]{:S(2)}) collective-permute-start(bf16[23,1024]{1,0:T(8,128)(2,1)S(1)} %slice.10), channel_id=1, source_target_pairs={{0,32},{32,64},{64,96},{96,128},{128,160},{160,192},{192,224},{224... | collective-permute-start | bytes 141320

commit v2 on v1

v2 whole, which is shorter than its diff:
```python
import functools

import jax
import jax.numpy as jnp
from jax import lax
from jax.experimental import pallas as pl
from jax.experimental.pallas import tpu as pltpu
from jax.sharding import PartitionSpec as P

DIGITS = 6
EXTRA = 16
VM = pl.BlockSpec(memory_space=pltpu.VMEM)


def from_behind(block, axis, distance):
    devices = range(lax.axis_size(axis))
    route = [(i - distance, i) for i in devices if i - distance in devices]
    return lax.ppermute(block, axis, route)


def pack_kernel(chips, rows, core_ref, mask_ref, normed_ref, grad_ref, own_ref, other_ref):
    tokens, width = normed_ref.shape
    lanes = own_ref.shape[1]
    count = jnp.sum(mask_ref[...])
    lane = lax.broadcasted_iota(jnp.int32, (EXTRA, grad_ref.shape[1]), 1)
    row = lax.broadcasted_iota(jnp.int32, (EXTRA, grad_ref.shape[1]), 0)
    digit = jnp.bitwise_and(jnp.right_shift(count, 3 * jnp.minimum(lane, DIGITS)), 7)
    digit = jnp.where((lane < DIGITS) & (row == 0), digit, 0).astype(jnp.float32).astype(jnp.bfloat16)
    at = lax.broadcasted_iota(jnp.int32, (EXTRA, lanes), 1)
    first = lax.broadcasted_iota(jnp.int32, (EXTRA, lanes), 0) == 0
    marks = first & (at % (rows + 1) == rows) & (at < chips * (rows + 1))
    marks = jnp.where(marks, 1.0, 0.0).astype(jnp.bfloat16)
    other_ref[:tokens, lanes:] = grad_ref[...]
    other_ref[tokens:, lanes:] = digit
    for ref in (own_ref, other_ref):
        ref[tokens:, :lanes] = marks

    def spread(parity, ref):
        pieces = []
        for j in range(chips):
            low = (2 * j + parity) * rows
            high = min(low + rows, width)
            pieces += [normed_ref[:, low:high], jnp.zeros((tokens, rows + 1 - (high - low)), jnp.bfloat16)]
        pieces.append(jnp.zeros((tokens, lanes - chips * (rows + 1)), jnp.bfloat16))
        ref[:tokens, :lanes] = jnp.concatenate(pieces, axis=1)

    @pl.when(core_ref[0] == 0)
    def _():
        spread(0, own_ref)
        spread(1, other_ref)

    @pl.when(core_ref[0] != 0)
    def _():
        spread(1, own_ref)
        spread(0, other_ref)


def pack(core, mask, inputs, upstream, chips, rows):
    lanes = -(-chips * (rows + 1) // 128) * 128
    height = inputs.shape[0] + EXTRA
    return pl.pallas_call(
        functools.partial(pack_kernel, chips, rows),
        out_shape=(
            jax.ShapeDtypeStruct((height, lanes), jnp.bfloat16),
            jax.ShapeDtypeStruct((height, lanes + upstream.shape[1]), jnp.bfloat16),
        ),
        in_specs=[pl.BlockSpec(memory_space=pltpu.SMEM)] + [VM] * 3,
        out_specs=(VM, VM),
        name="pack",
        compiler_params=pltpu.CompilerParams(vmem_limit_bytes=60 << 20),
        cost_estimate=pl.CostEstimate(flops=0, bytes_accessed=7 << 20, transcendentals=0),
    )(core, mask, inputs, upstream)


def term_kernel(own_ref, other_ref, partner_ref, out_ref):
    lanes = own_ref.shape[1]
    step = 256
    for m in range(0, out_ref.shape[0], step):
        size = min(step, out_ref.shape[0] - m)
        tile = sum(
            lax.dot_general(
                left[:, m : m + size], right[:, lanes:], (((0,), (0,)), ((), ())), preferred_element_type=jnp.float32
            )
            for left, right in ((own_ref, other_ref), (partner_ref, partner_ref))
        )
        out_ref[m : m + size, :] = tile.astype(jnp.bfloat16)


def terms(own, other, partner, rows, width):
    return pl.pallas_call(
        term_kernel,
        out_shape=jax.ShapeDtypeStruct((rows, width), jnp.bfloat16),
        in_specs=[VM] * 3,
        out_specs=VM,
        name="terms",
        compiler_params=pltpu.CompilerParams(vmem_limit_bytes=20 << 20),
        cost_estimate=pl.CostEstimate(flops=4 * own.shape[0] * rows * width, bytes_accessed=6 << 20, transcendentals=0),
    )(own, other, partner)


def product_kernel(grad_ref, weight_ref, out_ref, held_ref, arrived):
    parts, step = held_ref.shape[0], held_ref.shape[1]
    copies = [
        pltpu.make_async_copy(weight_ref.at[pl.ds(i * step, step)], held_ref.at[i], arrived.at[i]) for i in range(parts)
    ]
    for copy in copies:
        copy.start()
    for i, copy in enumerate(copies):
        copy.wait()
        out_ref[:, i * step : (i + 1) * step] = lax.dot_general(
            grad_ref[...], held_ref[i], (((1,), (1,)), ((), ())), preferred_element_type=jnp.float32
        ).astype(jnp.bfloat16)


def product(grad, weight):
    parts = 4
    step = weight.shape[0] // parts
    return pl.pallas_call(
        product_kernel,
        out_shape=jax.ShapeDtypeStruct((grad.shape[0], weight.shape[0]), jnp.bfloat16),
        in_specs=[VM, pl.BlockSpec(memory_space=pltpu.HBM)],
        out_specs=VM,
        scratch_shapes=[pltpu.VMEM((parts, step, weight.shape[1]), jnp.bfloat16), pltpu.SemaphoreType.DMA((parts,))],
        name="product",
        compiler_params=pltpu.CompilerParams(vmem_limit_bytes=55 << 20),
        cost_estimate=pl.CostEstimate(flops=2 * grad.size * weight.shape[0], bytes_accessed=7 << 20, transcendentals=0),
    )(grad, weight)


def finish_kernel(mine_ref, passed_ref, weight_out_ref, passed_out_ref, held_ref, done):
    rows = weight_out_ref.shape[0]
    digits = mine_ref[rows : rows + 1, :128].astype(jnp.float32)
    lane = lax.broadcasted_iota(jnp.int32, (1, 128), 1)
    scale = jnp.where(lane < DIGITS, jnp.left_shift(1, 3 * jnp.minimum(lane, DIGITS)), 0).astype(jnp.float32)
    inverse = 1.0 / jnp.sum(digits * scale)
    parts = held_ref.shape[0]
    step = passed_ref.shape[0] // parts
    copies = []
    for i in range(parts):
        held_ref[i] = (passed_ref[i * step : (i + 1) * step, :].astype(jnp.float32) * inverse).astype(jnp.bfloat16)
        copies.append(pltpu.make_async_copy(held_ref.at[i], passed_out_ref.at[pl.ds(i * step, step)], done.at[i]))
        copies[-1].start()
    for q in range(weight_out_ref.shape[1]):
        weight_out_ref[:, q, :] = mine_ref[:rows, 128 * q : 128 * (q + 1)].astype(jnp.float32) * inverse
    for copy in copies:
        copy.wait()


def finish(mine, passed):
    rows, parts = mine.shape[0] - 1, 4
    return pl.pallas_call(
        finish_kernel,
        out_shape=(
            jax.ShapeDtypeStruct((rows, mine.shape[1] // 128, 128), jnp.float32),
            jax.ShapeDtypeStruct(passed.shape, jnp.bfloat16),
        ),
        in_specs=[VM, VM],
        out_specs=(VM, pl.BlockSpec(memory_space=pltpu.HBM)),
        scratch_shapes=[
            pltpu.VMEM((parts, passed.shape[0] // parts, passed.shape[1]), jnp.bfloat16),
            pltpu.SemaphoreType.DMA((parts,)),
        ],
        name="finish",
        compiler_params=pltpu.CompilerParams(vmem_limit_bytes=20 << 20),
    )(mine, passed)


def local(normed, w_value, grad_value, assistant_mask):
    inputs = normed[0]
    weight = w_value[0]
    upstream = grad_value[0]
    n = lax.axis_size("dp")
    chips = n // 2
    rows = -(-inputs.shape[1] // n)
    core = lax.rem(lax.axis_index("dp"), 2).reshape(1)

    own, other = pack(core, assistant_mask[0], inputs, upstream, chips, rows)
    partner = lax.ppermute(other, "dp", [(i, i ^ 1) for i in range(n)])
    upstream, _ = lax.optimization_barrier((upstream, other))
    passed = from_behind(product(upstream, weight), "pipe", -1)
    term = terms(own, other, partner, chips * (rows + 1), upstream.shape[1])
    parity = [[2 * z + c for z in range(chips)] for c in range(2)]
    mine = lax.psum_scatter(term, "dp", scatter_dimension=0, tiled=True, axis_index_groups=parity)
    weight_grad, input_grad = finish(mine, passed)
    return (weight_grad.reshape(1, 1, rows, -1), input_grad[None])


def solution(mesh):
    return jax.shard_map(
        local,
        mesh=mesh,
        in_specs=(
            P("pipe", "dp", "tensor"),
            P("pipe", "tensor", None),
            P("pipe", "dp", None),
            P("dp", None, None),
        ),
        out_specs=(P("pipe", "tensor", "dp", None), P("pipe", "dp", "tensor")),
        check_vma=False,
    )
```

time: 83.2 us -> 72.1 us (0.87); the launches traced: 81.9 us -> 71.8 us
  blocking collectives: 55.2 us -> 30.3 us
  starting transfers between devices: 4.31 us -> 15.7 us
  Pallas kernels: 7.46 us -> 17.7 us
  matrix products: 5.83 us -> 0 us
  waiting for transfers between devices: 0.58 us -> 5.09 us
  other arithmetic: 3.78 us -> 0 us
  local copies, waits for them, and re-layouts: 3.38 us -> 1.63 us
    unnamed x1, blocking collectives: 55.2 us -> 30.3 us
    ppermute x0 -> x1, starting transfers between devices: none -> 12.3 us  [local(): partner = lax.ppermute(other, 'dp', [(i, i ^ 1) for i in range(n)])]
    pallas_call x1 -> x4, Pallas kernels: 7.46 us -> 17.7 us  [the longest x1 6.52 us: product(): pl.pallas_call(product_kernel, out_shape=jax.ShapeDtypeStruct((grad.shape...]
    dot_general x1 -> x0, matrix products: 5.83 us -> none  [local(): lax.dot_general(upstream, weight, (((1,), (1,)), ((), ())), preferred_ele...]
    ppermute x1, waiting for transfers between devices: 0.01 us -> 5.08 us  [from_behind(): return lax.ppermute(block, axis, route)]
    broadcast_in_dim x2 -> x0, other arithmetic: 3.05 us -> none  [local(): return (weight_grad[None, None], input_grad[None])]
    unnamed x6 -> x8, local copies, waits for them, and re-layouts: 2.64 us -> 1.63 us
    unnamed x1, starting transfers between devices: 3.03 us -> 2.11 us
  transfers between devices with their start and end apart: 2 -> 3, of which waited for: 1 -> 1; matrix products, arithmetic and copies ran while one was open for 73% -> 44% of each run, Pallas kernels for 9% -> 13%
where the time goes in v2:
time: 72.1 us; the launch traced here: 71.8 us
  blocking collectives  30.3 us (42%)
  Pallas kernels  17.7 us (25%)
  starting transfers between devices  15.7 us (22%)
  waiting for transfers between devices  5.09 us (7%)
  local copies, waits for them, and re-layouts  1.63 us (2%)
  between operations  1.4 us (2%)
    unnamed x1, blocking collectives  30.3 us
    ppermute x1, starting transfers between devices, local(): partner = lax.ppermute(other, 'dp', [(i, i ^ 1) for i in range(n)])  12.3 us
    pallas_call x1, Pallas kernels, product(): pl.pallas_call(product_kernel, out_shape=jax.ShapeDtypeStruct((grad.shape...  6.52 us
    ppermute x1, waiting for transfers between devices, from_behind(): return lax.ppermute(block, axis, route)  5.08 us
    pallas_call x1, Pallas kernels, pack(): pl.pallas_call(functools.partial(pack_kernel, chips, rows), out_shape=(ja...  4.76 us
    pallas_call x1, Pallas kernels, finish(): pl.pallas_call(finish_kernel, out_shape=(jax.ShapeDtypeStruct((rows, mine...  3.76 us
    pallas_call x1, Pallas kernels, terms(): pl.pallas_call(term_kernel, out_shape=jax.ShapeDtypeStruct((rows, width),...  2.65 us
    unnamed x1, starting transfers between devices  2.11 us
  transfers between devices with their start and end apart: 3, of which 1 were waited for; matrix products, arithmetic and copies ran while one was open for 44% of the time, Pallas kernels for 13%

profile of v2, /device:TPU:1, one launch (start us, length us, event | category | flops | bytes accessed | tf_op | source)
XLA Modules:
  0.0 71.8 jit_solution(11301881656189865308)
XLA Ops:
  0.6 4.8 %pack.1 = (bf16[464,1152]{1,0:T(8,128)(2,1)}, bf16[464,2176]{1,0:T(8,128)(2,1)}) custom-call(s32[1]{0:T(128)} %bitcast.core_ref, s32[4,8192]{1,0:T(4,128)} %bitcast.13, bf16[448,2048]{1,0:T(8,128)(2,1)} %bitcast.10, bf16[448,1024]{1,0:T(8,128)(2,1)} %bitcast.11), custom_call_target="tpu_custom_call" | custom-call | bytes 7340032 | tf_op jit(solution)/shard_map/pack/pallas_call | solution.py:61
  5.4 12.3 %collective-permute-start = (bf16[464,2176]{1,0:T(8,128)(2,1)}, bf16[464,2176]{1,0:T(8,128)(2,1)S(1)}, u32[]{:S(2)}, u32[]{:S(2)}) collective-permute-start(bf16[464,2176]{1,0:T(8,128)(2,1)} %get-tuple-element.8.other_ref), channel_id=1, source_target_pairs={{0,32},{32,0},{64,96},{96,64},{128,160},{160,128},{192,224},{224,1... | collective-permute-start | bytes 6057992 | tf_op jit(solution)/shard_map/ppermute | solution.py:178
  17.7 0.0 copy-start
  17.8 0.0 copy-start.1
  17.8 6.5 %product.1 = bf16[448,2048]{1,0:T(8,128)(2,1)} custom-call(bf16[448,1024]{1,0:T(8,128)(2,1)} %bitcast.12, bf16[2048,1024]{1,0:T(8,128)(2,1)} %bitcast.14), custom_call_target="tpu_custom_call" | custom-call | flops 1879048192 | bytes 7340032 | tf_op jit(solution)/shard_map/product/pallas_call | solution.py:118
  24.3 1.3 %collective-permute-start.1 = (bf16[448,2048]{1,0:T(8,128)(2,1)}, bf16[448,2048]{1,0:T(8,128)(2,1)}, u32[]{:S(2)}, u32[]{:S(2)}) collective-permute-start(bf16[448,2048]{1,0:T(8,128)(2,1)} %product.1), channel_id=1, source_target_pairs={{1,0},{2,1},{3,2},{5,4},{6,5},{7,6},{9,8},{10,9},{11,10},{13,12},{... | collective-permute-start | bytes 5505032 | tf_op jit(solution)/shard_map/ppermute | solution.py:18
  25.6 0.0 collective-permute-done.partner_ref
  25.6 0.0 copy-done
  25.6 0.0 copy-done.1
  25.6 2.7 %terms.1 = bf16[1044,1024]{1,0:T(8,128)(2,1)S(1)} custom-call(bf16[464,1152]{1,0:T(8,128)(2,1)S(1)} %copy-done.1, bf16[464,2176]{1,0:T(8,128)(2,1)S(1)} %copy-done, bf16[464,2176]{1,0:T(8,128)(2,1)S(1)} %collective-permute-done.partner_ref), custom_call_target="tpu_custom_call" | custom-call | flops 1984167936 | bytes 6291456 | tf_op jit(solution)/shard_map/terms/pallas_call | solution.py:90
  28.3 30.3 %fusion = bf16[88,1024]{1,0:T(8,128)(2,1)S(1)} fusion(bf16[1044,1024]{1,0:T(8,128)(2,1)S(1)} %terms.1), kind=kCustom, calls=%all-reduce-scatter | all-reduce-scatter fusion | flops 1081345 | bytes 2322432
  58.6 2.1 %collective-permute-start.2 = (bf16[11,1024]{1,0:T(8,128)(2,1)S(1)}, bf16[11,1024]{1,0:T(8,128)(2,1)S(1)}, u32[]{:S(2)}, u32[]{:S(2)}) collective-permute-start(bf16[11,1024]{1,0:T(8,128)(2,1)S(1)} %slice), channel_id=1, source_target_pairs={{0,64},{64,128},{128,192},{192,256},{256,320},{320,384},{384,448},... | collective-permute-start | bytes 67592
  60.7 1.3 %dynamic-slice.4 = u32[1]{0:T(128)} dynamic-slice(u32[768]{0:T(1024)} %constant.16, u32[]{:S(6)} %partition-id.4), dynamic_slice_sizes={1} | dynamic-slice | bytes 12
  62.6 0.0 collective-permute-done.2
  62.6 0.3 concatenate
  62.9 0.1 constant_dynamic-slice_fusion.mine_ref
  63.0 5.1 %collective-permute-done.1.passed_ref = bf16[448,2048]{1,0:T(8,128)(2,1)} collective-permute-done((bf16[448,2048]{1,0:T(8,128)(2,1)}, bf16[448,2048]{1,0:T(8,128)(2,1)}, u32[]{:S(2)}, u32[]{:S(2)}) %collective-permute-start.1) | collective-permute-done | bytes 1835040 | tf_op jit(solution)/shard_map/ppermute | solution.py:18
  68.1 3.8 %finish.1 = (f32[86,8,128]{2,1,0:T(8,128)}, bf16[448,2048]{1,0:T(8,128)(2,1)}) custom-call(bf16[87,1024]{1,0:T(8,128)(2,1)S(1)} %constant_dynamic-slice_fusion.mine_ref, bf16[448,2048]{1,0:T(8,128)(2,1)} %collective-permute-done.1.passed_ref), custom_call_target="tpu_custom_call" | custom-call | tf_op jit(solution)/shard_map/finish/pallas_call | solution.py:151
  (1 shorter events, 0.0 us)
Async XLA Ops:
  5.4 20.2 %collective-permute-start = (bf16[464,2176]{1,0:T(8,128)(2,1)}, bf16[464,2176]{1,0:T(8,128)(2,1)S(1)}, u32[]{:S(2)}, u32[]{:S(2)}) collective-permute-start(bf16[464,2176]{1,0:T(8,128)(2,1)} %get-tuple-element.8.other_ref), channel_id=1, source_target_pairs={{0,32},{32,0},{64,96},{96,64},{128,160},{160,128},{192,224},{224,1... | collective-permute-start | bytes 6057992 | tf_op jit(solution)/shard_map/ppermute | solution.py:178
  17.7 7.9 %copy-start = (bf16[464,2176]{1,0:T(8,128)(2,1)S(1)}, bf16[464,2176]{1,0:T(8,128)(2,1)}, u32[]{:S(2)}) copy-start(bf16[464,2176]{1,0:T(8,128)(2,1)} %get-tuple-element.8.other_ref) | copy-start | bytes 6057988
  17.8 7.9 %copy-start.1 = (bf16[464,1152]{1,0:T(8,128)(2,1)S(1)}, bf16[464,1152]{1,0:T(8,128)(2,1)}, u32[]{:S(2)}) copy-start(bf16[464,1152]{1,0:T(8,128)(2,1)} %get-tuple-element.7.own_ref) | copy-start | bytes 3207172
  24.3 43.8 %collective-permute-start.1 = (bf16[448,2048]{1,0:T(8,128)(2,1)}, bf16[448,2048]{1,0:T(8,128)(2,1)}, u32[]{:S(2)}, u32[]{:S(2)}) collective-permute-start(bf16[448,2048]{1,0:T(8,128)(2,1)} %product.1), channel_id=1, source_target_pairs={{1,0},{2,1},{3,2},{5,4},{6,5},{7,6},{9,8},{10,9},{11,10},{13,12},{... | collective-permute-start | bytes 5505032 | tf_op jit(solution)/shard_map/ppermute | solution.py:18
  58.6 4.0 %collective-permute-start.2 = (bf16[11,1024]{1,0:T(8,128)(2,1)S(1)}, bf16[11,1024]{1,0:T(8,128)(2,1)S(1)}, u32[]{:S(2)}, u32[]{:S(2)}) collective-permute-start(bf16[11,1024]{1,0:T(8,128)(2,1)S(1)} %slice), channel_id=1, source_target_pairs={{0,64},{64,128},{128,192},{192,256},{256,320},{320,384},{384,448},... | collective-permute-start | bytes 67592

commit v3 on v2

v3 whole, which is shorter than its diff:
```python
import functools

import jax
import jax.numpy as jnp
from jax import lax
from jax.experimental import pallas as pl
from jax.experimental.pallas import tpu as pltpu
from jax.sharding import PartitionSpec as P

DIGITS = 6
EXTRA = 16
PARTS = 4
VM = pl.BlockSpec(memory_space=pltpu.VMEM)
ANY = pl.BlockSpec(memory_space=pl.ANY)


def from_behind(block, axis, distance):
    devices = range(lax.axis_size(axis))
    route = [(i - distance, i) for i in devices if i - distance in devices]
    return lax.ppermute(block, axis, route)


def pack_kernel(
    chips, rows, core_ref, mask_ref, normed_ref, grad_ref, own_ref, other_ref, mask, normed, own, other, arrived, left
):
    tokens, width = normed.shape
    lanes, columns = own.shape[1], grad_ref.shape[1]
    parts = PARTS
    step = tokens // parts
    loads = [pltpu.make_async_copy(mask_ref, mask, arrived.at[2 * parts])]
    for i in range(parts):
        at = pl.ds(i * step, step)
        loads.append(pltpu.make_async_copy(normed_ref.at[at], normed.at[at], arrived.at[2 * i]))
        loads.append(pltpu.make_async_copy(grad_ref.at[at], other.at[at, pl.ds(lanes, columns)], arrived.at[2 * i + 1]))
    for load in loads:
        load.start()

    loads[0].wait()
    count = jnp.sum(mask[...])
    lane = lax.broadcasted_iota(jnp.int32, (EXTRA, columns), 1)
    row = lax.broadcasted_iota(jnp.int32, (EXTRA, columns), 0)
    digit = jnp.bitwise_and(jnp.right_shift(count, 3 * jnp.minimum(lane, DIGITS)), 7)
    digit = jnp.where((lane < DIGITS) & (row == 0), digit, 0).astype(jnp.float32).astype(jnp.bfloat16)
    at = lax.broadcasted_iota(jnp.int32, (EXTRA, lanes), 1)
    first = lax.broadcasted_iota(jnp.int32, (EXTRA, lanes), 0) == 0
    marks = first & (at % (rows + 1) == rows) & (at < chips * (rows + 1))
    marks = jnp.where(marks, 1.0, 0.0).astype(jnp.bfloat16)
    other[tokens:, lanes:] = digit
    other[tokens:, :lanes] = marks
    own[tokens:, :] = marks

    def spread(low, parity, ref):
        pieces = []
        for j in range(chips):
            begin = (2 * j + parity) * rows
            end = min(begin + rows, width)
            pieces += [normed[low : low + step, begin:end], jnp.zeros((step, rows + 1 - (end - begin)), jnp.bfloat16)]
        pieces.append(jnp.zeros((step, lanes - chips * (rows + 1)), jnp.bfloat16))
        ref[low : low + step, :lanes] = jnp.concatenate(pieces, axis=1)

    stores = []
    for i in range(parts):
        loads[2 * i + 1].wait()
        loads[2 * i + 2].wait()
        for core in range(2):

            @pl.when(core_ref[0] == core)
            def _():
                spread(i * step, core, own)
                spread(i * step, 1 - core, other)

        at = pl.ds(i * step, step if i < parts - 1 else step + EXTRA)
        stores.append(pltpu.make_async_copy(other.at[at], other_ref.at[at], left.at[2 * i]))
        stores.append(pltpu.make_async_copy(own.at[at], own_ref.at[at], left.at[2 * i + 1]))
        stores[-2].start()
        stores[-1].start()
    for store in stores:
        store.wait()


def pack(core, mask, inputs, upstream, chips, rows):
    lanes = -(-chips * (rows + 1) // 128) * 128
    height = inputs.shape[0] + EXTRA
    own = jax.ShapeDtypeStruct((height, lanes), jnp.bfloat16)
    other = jax.ShapeDtypeStruct((height, lanes + upstream.shape[1]), jnp.bfloat16)
    return pl.pallas_call(
        functools.partial(pack_kernel, chips, rows),
        out_shape=(own, other),
        in_specs=[pl.BlockSpec(memory_space=pltpu.SMEM)] + [ANY] * 3,
        out_specs=(ANY, ANY),
        scratch_shapes=[
            pltpu.VMEM(mask.shape, mask.dtype),
            pltpu.VMEM(inputs.shape, inputs.dtype),
            pltpu.VMEM(own.shape, own.dtype),
            pltpu.VMEM(other.shape, other.dtype),
            pltpu.SemaphoreType.DMA((2 * PARTS + 1,)),
            pltpu.SemaphoreType.DMA((2 * PARTS,)),
        ],
        name="pack",
        compiler_params=pltpu.CompilerParams(vmem_limit_bytes=60 << 20),
        cost_estimate=pl.CostEstimate(flops=0, bytes_accessed=7 << 20, transcendentals=0),
    )(core, mask, inputs, upstream)


def term_kernel(own_ref, other_ref, partner_ref, out_ref):
    lanes = own_ref.shape[1]
    step = 256
    for m in range(0, out_ref.shape[0], step):
        size = min(step, out_ref.shape[0] - m)
        tile = sum(
            lax.dot_general(
                left[:, m : m + size], right[:, lanes:], (((0,), (0,)), ((), ())), preferred_element_type=jnp.float32
            )
            for left, right in ((own_ref, other_ref), (partner_ref, partner_ref))
        )
        out_ref[m : m + size, :] = tile.astype(jnp.bfloat16)


def terms(own, other, partner, rows, width):
    return pl.pallas_call(
        term_kernel,
        out_shape=jax.ShapeDtypeStruct((rows, width), jnp.bfloat16),
        in_specs=[VM] * 3,
        out_specs=VM,
        name="terms",
        compiler_params=pltpu.CompilerParams(vmem_limit_bytes=20 << 20),
        cost_estimate=pl.CostEstimate(flops=4 * own.shape[0] * rows * width, bytes_accessed=6 << 20, transcendentals=0),
    )(own, other, partner)


def product_kernel(grad_ref, weight_ref, out_ref, grad, weight, out, arrived, left):
    parts, step = weight.shape[0], weight.shape[1]
    loads = [pltpu.make_async_copy(grad_ref, grad, arrived.at[parts])]
    for i in range(parts):
        loads.append(pltpu.make_async_copy(weight_ref.at[pl.ds(i * step, step)], weight.at[i], arrived.at[i]))
    for load in loads:
        load.start()
    loads[0].wait()
    stores = []
    for i in range(parts):
        loads[i + 1].wait()
        out[i] = lax.dot_general(
            grad[...], weight[i], (((1,), (1,)), ((), ())), preferred_element_type=jnp.float32
        ).astype(jnp.bfloat16)
        stores.append(pltpu.make_async_copy(out.at[i], out_ref.at[:, pl.ds(i * step, step)], left.at[i]))
        stores[-1].start()
    for store in stores:
        store.wait()


def product(grad, weight):
    tokens, width = grad.shape[0], weight.shape[0]
    step = width // PARTS
    return pl.pallas_call(
        product_kernel,
        out_shape=jax.ShapeDtypeStruct((tokens, width), jnp.bfloat16),
        in_specs=[ANY, ANY],
        out_specs=ANY,
        scratch_shapes=[
            pltpu.VMEM(grad.shape, grad.dtype),
            pltpu.VMEM((PARTS, step, weight.shape[1]), weight.dtype),
            pltpu.VMEM((PARTS, tokens, step), jnp.bfloat16),
            pltpu.SemaphoreType.DMA((PARTS + 1,)),
            pltpu.SemaphoreType.DMA((PARTS,)),
        ],
        name="product",
        compiler_params=pltpu.CompilerParams(vmem_limit_bytes=55 << 20),
        cost_estimate=pl.CostEstimate(flops=2 * grad.size * width, bytes_accessed=7 << 20, transcendentals=0),
    )(grad, weight)


def finish_kernel(mine_ref, passed_ref, weight_out_ref, passed_out_ref, mine, passed, weight_out, arrived, left):
    rows = weight_out_ref.shape[0]
    parts = PARTS
    step = passed.shape[0] // parts
    loads = [pltpu.make_async_copy(mine_ref, mine, arrived.at[parts])]
    for i in range(parts):
        at = pl.ds(i * step, step)
        loads.append(pltpu.make_async_copy(passed_ref.at[at], passed.at[at], arrived.at[i]))
    for load in loads:
        load.start()
    loads[0].wait()
    digits = mine[rows : rows + 1, :128].astype(jnp.float32)
    lane = lax.broadcasted_iota(jnp.int32, (1, 128), 1)
    scale = jnp.where(lane < DIGITS, jnp.left_shift(1, 3 * jnp.minimum(lane, DIGITS)), 0).astype(jnp.float32)
    inverse = 1.0 / jnp.sum(digits * scale)
    for q in range(weight_out_ref.shape[1]):
        weight_out[:, q, :] = mine[:rows, 128 * q : 128 * (q + 1)].astype(jnp.float32) * inverse
    stores = [pltpu.make_async_copy(weight_out, weight_out_ref, left.at[parts])]
    stores[0].start()
    for i in range(parts):
        at = pl.ds(i * step, step)
        loads[i + 1].wait()
        passed[at, :] = (passed[at, :].astype(jnp.float32) * inverse).astype(jnp.bfloat16)
        stores.append(pltpu.make_async_copy(passed.at[at], passed_out_ref.at[at], left.at[i]))
        stores[-1].start()
    for store in stores:
        store.wait()


def finish(mine, passed):
    weight_out = jax.ShapeDtypeStruct((mine.shape[0] - 1, mine.shape[1] // 128, 128), jnp.float32)
    return pl.pallas_call(
        finish_kernel,
        out_shape=(weight_out, jax.ShapeDtypeStruct(passed.shape, jnp.bfloat16)),
        in_specs=[ANY, ANY],
        out_specs=(ANY, ANY),
        scratch_shapes=[
            pltpu.VMEM(mine.shape, mine.dtype),
            pltpu.VMEM(passed.shape, passed.dtype),
            pltpu.VMEM(weight_out.shape, weight_out.dtype),
            pltpu.SemaphoreType.DMA((PARTS + 1,)),
            pltpu.SemaphoreType.DMA((PARTS + 1,)),
        ],
        name="finish",
        compiler_params=pltpu.CompilerParams(vmem_limit_bytes=20 << 20),
    )(mine, passed)


def local(normed, w_value, grad_value, assistant_mask):
    inputs = normed[0]
    weight = w_value[0]
    upstream = grad_value[0]
    n = lax.axis_size("dp")
    chips = n // 2
    rows = -(-inputs.shape[1] // n)
    core = lax.rem(lax.axis_index("dp"), 2).reshape(1)

    own, other = pack(core, assistant_mask[0], inputs, upstream, chips, rows)
    partner = lax.ppermute(other, "dp", [(i, i ^ 1) for i in range(n)])
    upstream, _ = lax.optimization_barrier((upstream, other))
    passed = from_behind(product(upstream, weight), "pipe", -1)
    term = terms(own, other, partner, chips * (rows + 1), upstream.shape[1])
    parity = [[2 * z + c for z in range(chips)] for c in range(2)]
    mine = lax.psum_scatter(term, "dp", scatter_dimension=0, tiled=True, axis_index_groups=parity)
    weight_grad, input_grad = finish(mine, passed)
    return (weight_grad.reshape(1, 1, rows, -1), input_grad[None])


def solution(mesh):
    return jax.shard_map(
        local,
        mesh=mesh,
        in_specs=(
            P("pipe", "dp", "tensor"),
            P("pipe", "tensor", None),
            P("pipe", "dp", None),
            P("dp", None, None),
        ),
        out_specs=(P("pipe", "tensor", "dp", None), P("pipe", "dp", "tensor")),
        check_vma=False,
    )
```

time: 72.1 us -> 68.7 us (0.953)
  Pallas kernels: 17.7 us -> 14.2 us
    pallas_call x3, Pallas kernels: 15 us -> 11.5 us  [the longest x1 5.2 us: product(): pl.pallas_call(product_kernel, out_shape=jax.ShapeDtypeStruct((tokens, wi...]
  transfers between devices with their start and end apart: 3 -> 3, of which waited for: 1 -> 1; matrix products, arithmetic and copies ran while one was open for 44% -> 47% of each run, Pallas kernels for 13% -> 11%
where the time goes in v3:
time: 68.7 us; the launch traced here: 68.4 us
  blocking collectives  30.3 us (44%)
  starting transfers between devices  15.7 us (23%)
  Pallas kernels  14.2 us (21%)
  waiting for transfers between devices  5.09 us (7%)
  local copies, waits for them, and re-layouts  1.63 us (2%)
  between operations  1.41 us (2%)
    unnamed x1, blocking collectives  30.3 us
    ppermute x1, starting transfers between devices, local(): partner = lax.ppermute(other, 'dp', [(i, i ^ 1) for i in range(n)])  12.4 us
    pallas_call x1, Pallas kernels, product(): pl.pallas_call(product_kernel, out_shape=jax.ShapeDtypeStruct((tokens, wi...  5.2 us
    ppermute x1, waiting for transfers between devices, from_behind(): return lax.ppermute(block, axis, route)  5.09 us
    pallas_call x1, Pallas kernels, pack(): pl.pallas_call(functools.partial(pack_kernel, chips, rows), out_shape=(ow...  3.65 us
    pallas_call x1, Pallas kernels, finish(): pl.pallas_call(finish_kernel, out_shape=(weight_out, jax.ShapeDtypeStruct...  2.69 us
    pallas_call x1, Pallas kernels, terms(): pl.pallas_call(term_kernel, out_shape=jax.ShapeDtypeStruct((rows, width),...  2.65 us
    unnamed x1, starting transfers between devices  2.06 us
  transfers between devices with their start and end apart: 3, of which 1 were waited for; matrix products, arithmetic and copies ran while one was open for 47% of the time, Pallas kernels for 11%

profile of v3, /device:TPU:1, one launch (start us, length us, event | category | flops | bytes accessed | tf_op | source)
XLA Modules:
  0.0 68.4 jit_solution(5554766672972849971)
XLA Ops:
  0.6 3.6 %pack.1 = (bf16[464,1152]{1,0:T(8,128)(2,1)}, bf16[464,2176]{1,0:T(8,128)(2,1)}) custom-call(s32[1]{0:T(128)} %bitcast.core_ref, s32[4,8192]{1,0:T(4,128)} %bitcast.13, bf16[448,2048]{1,0:T(8,128)(2,1)} %bitcast.10, bf16[448,1024]{1,0:T(8,128)(2,1)} %bitcast.11), custom_call_target="tpu_custom_call" | custom-call | bytes 7340032 | tf_op jit(solution)/shard_map/pack/pallas_call | solution.py:86
  4.3 12.4 %collective-permute-start = (bf16[464,2176]{1,0:T(8,128)(2,1)}, bf16[464,2176]{1,0:T(8,128)(2,1)S(1)}, u32[]{:S(2)}, u32[]{:S(2)}) collective-permute-start(bf16[464,2176]{1,0:T(8,128)(2,1)} %get-tuple-element.8.other_ref), channel_id=1, source_target_pairs={{0,32},{32,0},{64,96},{96,64},{128,160},{160,128},{192,224},{224,1... | collective-permute-start | bytes 6057992 | tf_op jit(solution)/shard_map/ppermute | solution.py:230
  16.7 0.0 copy-start
  16.7 0.0 copy-start.1
  16.7 5.2 %product.1 = bf16[448,2048]{1,0:T(8,128)(2,1)} custom-call(bf16[448,1024]{1,0:T(8,128)(2,1)} %bitcast.12, bf16[2048,1024]{1,0:T(8,128)(2,1)} %bitcast.14), custom_call_target="tpu_custom_call" | custom-call | flops 1879048192 | bytes 7340032 | tf_op jit(solution)/shard_map/product/pallas_call | solution.py:154
  21.9 1.3 %collective-permute-start.1 = (bf16[448,2048]{1,0:T(8,128)(2,1)}, bf16[448,2048]{1,0:T(8,128)(2,1)}, u32[]{:S(2)}, u32[]{:S(2)}) collective-permute-start(bf16[448,2048]{1,0:T(8,128)(2,1)} %product.1), channel_id=1, source_target_pairs={{1,0},{2,1},{3,2},{5,4},{6,5},{7,6},{9,8},{10,9},{11,10},{13,12},{... | collective-permute-start | bytes 5505032 | tf_op jit(solution)/shard_map/ppermute | solution.py:20
  23.2 0.0 collective-permute-done.partner_ref
  23.2 0.0 copy-done
  23.2 0.0 copy-done.1
  23.3 2.7 %terms.1 = bf16[1044,1024]{1,0:T(8,128)(2,1)S(1)} custom-call(bf16[464,1152]{1,0:T(8,128)(2,1)S(1)} %copy-done.1, bf16[464,2176]{1,0:T(8,128)(2,1)S(1)} %copy-done, bf16[464,2176]{1,0:T(8,128)(2,1)S(1)} %collective-permute-done.partner_ref), custom_call_target="tpu_custom_call" | custom-call | flops 1984167936 | bytes 6291456 | tf_op jit(solution)/shard_map/terms/pallas_call | solution.py:120
  25.9 30.3 %fusion = bf16[88,1024]{1,0:T(8,128)(2,1)S(1)} fusion(bf16[1044,1024]{1,0:T(8,128)(2,1)S(1)} %terms.1), kind=kCustom, calls=%all-reduce-scatter | all-reduce-scatter fusion | flops 1081345 | bytes 2322432
  56.2 2.1 %collective-permute-start.2 = (bf16[11,1024]{1,0:T(8,128)(2,1)S(1)}, bf16[11,1024]{1,0:T(8,128)(2,1)S(1)}, u32[]{:S(2)}, u32[]{:S(2)}) collective-permute-start(bf16[11,1024]{1,0:T(8,128)(2,1)S(1)} %slice), channel_id=1, source_target_pairs={{0,64},{64,128},{128,192},{192,256},{256,320},{320,384},{384,448},... | collective-permute-start | bytes 67592
  58.3 1.3 %dynamic-slice.4 = u32[1]{0:T(128)} dynamic-slice(u32[768]{0:T(1024)} %constant.16, u32[]{:S(6)} %partition-id.4), dynamic_slice_sizes={1} | dynamic-slice | bytes 12
  60.2 0.0 collective-permute-done.2
  60.3 0.3 concatenate
  60.5 0.1 constant_dynamic-slice_fusion.mine_ref
  60.6 5.1 %collective-permute-done.1.passed_ref = bf16[448,2048]{1,0:T(8,128)(2,1)} collective-permute-done((bf16[448,2048]{1,0:T(8,128)(2,1)}, bf16[448,2048]{1,0:T(8,128)(2,1)}, u32[]{:S(2)}, u32[]{:S(2)}) %collective-permute-start.1) | collective-permute-done | bytes 1835040 | tf_op jit(solution)/shard_map/ppermute | solution.py:20
  65.7 2.7 %finish.1 = (f32[86,8,128]{2,1,0:T(8,128)}, bf16[448,2048]{1,0:T(8,128)(2,1)}) custom-call(bf16[87,1024]{1,0:T(8,128)(2,1)S(1)} %constant_dynamic-slice_fusion.mine_ref, bf16[448,2048]{1,0:T(8,128)(2,1)} %collective-permute-done.1.passed_ref), custom_call_target="tpu_custom_call" | custom-call | tf_op jit(solution)/shard_map/finish/pallas_call | solution.py:203
  (1 shorter events, 0.0 us)
Async XLA Ops:
  4.3 18.9 %collective-permute-start = (bf16[464,2176]{1,0:T(8,128)(2,1)}, bf16[464,2176]{1,0:T(8,128)(2,1)S(1)}, u32[]{:S(2)}, u32[]{:S(2)}) collective-permute-start(bf16[464,2176]{1,0:T(8,128)(2,1)} %get-tuple-element.8.other_ref), channel_id=1, source_target_pairs={{0,32},{32,0},{64,96},{96,64},{128,160},{160,128},{192,224},{224,1... | collective-permute-start | bytes 6057992 | tf_op jit(solution)/shard_map/ppermute | solution.py:230
  16.7 6.5 %copy-start = (bf16[464,2176]{1,0:T(8,128)(2,1)S(1)}, bf16[464,2176]{1,0:T(8,128)(2,1)}, u32[]{:S(2)}) copy-start(bf16[464,2176]{1,0:T(8,128)(2,1)} %get-tuple-element.8.other_ref) | copy-start | bytes 6057988
  16.7 6.5 %copy-start.1 = (bf16[464,1152]{1,0:T(8,128)(2,1)S(1)}, bf16[464,1152]{1,0:T(8,128)(2,1)}, u32[]{:S(2)}) copy-start(bf16[464,1152]{1,0:T(8,128)(2,1)} %get-tuple-element.7.own_ref) | copy-start | bytes 3207172
  21.9 43.8 %collective-permute-start.1 = (bf16[448,2048]{1,0:T(8,128)(2,1)}, bf16[448,2048]{1,0:T(8,128)(2,1)}, u32[]{:S(2)}, u32[]{:S(2)}) collective-permute-start(bf16[448,2048]{1,0:T(8,128)(2,1)} %product.1), channel_id=1, source_target_pairs={{1,0},{2,1},{3,2},{5,4},{6,5},{7,6},{9,8},{10,9},{11,10},{13,12},{... | collective-permute-start | bytes 5505032 | tf_op jit(solution)/shard_map/ppermute | solution.py:20
  56.2 4.0 %collective-permute-start.2 = (bf16[11,1024]{1,0:T(8,128)(2,1)S(1)}, bf16[11,1024]{1,0:T(8,128)(2,1)S(1)}, u32[]{:S(2)}, u32[]{:S(2)}) collective-permute-start(bf16[11,1024]{1,0:T(8,128)(2,1)S(1)} %slice), channel_id=1, source_target_pairs={{0,64},{64,128},{128,192},{192,256},{256,320},{320,384},{384,448},... | collective-permute-start | bytes 67592

commit v4 on v0

v4 whole, which is shorter than its diff:
```python
import functools

import jax
import jax.numpy as jnp
from jax import lax
from jax.experimental import pallas as pl
from jax.experimental.pallas import tpu as pltpu
from jax.sharding import PartitionSpec as P

DIGITS = 6
EXTRA = 16
TILE = 256
PARTS = 4
VM = pl.BlockSpec(memory_space=pltpu.VMEM)
ANY = pl.BlockSpec(memory_space=pl.ANY)


def from_behind(block, axis, distance):
    devices = range(lax.axis_size(axis))
    route = [(i - distance, i) for i in devices if i - distance in devices]
    return lax.ppermute(block, axis, route)


def front_kernel(
    chips, rows, core_ref, mask_ref, normed_ref, grad_ref, weight_ref, own_ref, other_ref, low_ref, high_ref,
    mask, normed, grad, weight, packs, product, arrived, left,
):
    tokens, width = normed.shape
    lanes, columns = own_ref.shape[1], grad_ref.shape[1]
    step, slab = tokens // PARTS, width // PARTS
    loads = [
        pltpu.make_async_copy(grad_ref, grad.at[pl.ds(0, tokens)], arrived.at[0]),
        pltpu.make_async_copy(mask_ref, mask, arrived.at[1]),
    ]
    for i in range(PARTS):
        at = pl.ds(i * step, step)
        loads.append(pltpu.make_async_copy(weight_ref.at[pl.ds(i * slab, slab)], weight.at[i], arrived.at[2 * i + 2]))
        loads.append(pltpu.make_async_copy(normed_ref.at[at], normed.at[at], arrived.at[2 * i + 3]))
    for load in loads:
        load.start()

    at = lax.broadcasted_iota(jnp.int32, (EXTRA, lanes), 1)
    first = lax.broadcasted_iota(jnp.int32, (EXTRA, lanes), 0) == 0
    marks = first & (at % (rows + 1) == rows) & (at < chips * (rows + 1))
    marks = jnp.where(marks, 1.0, 0.0).astype(jnp.bfloat16)
    for parity in range(2):
        packs[parity, tokens:, :] = marks
    lane = lax.broadcasted_iota(jnp.int32, (EXTRA, columns), 1)
    row = lax.broadcasted_iota(jnp.int32, (EXTRA, columns), 0)
    loads[0].wait()
    loads[1].wait()
    count = jnp.sum(mask[...])
    digit = jnp.bitwise_and(jnp.right_shift(count, 3 * jnp.minimum(lane, DIGITS)), 7)
    digit = jnp.where((lane < DIGITS) & (row == 0), digit, 0).astype(jnp.float32).astype(jnp.bfloat16)
    grad[tokens:, :] = digit
    core = core_ref[0]
    stores = [pltpu.make_async_copy(grad, other_ref.at[:, pl.ds(lanes, columns)], left.at[0])]
    stores[0].start()

    for i in range(PARTS):
        loads[2 * i + 2].wait()
        loads[2 * i + 3].wait()
        product[i] = lax.dot_general(
            grad[:tokens, :], weight[i], (((1,), (1,)), ((), ())), preferred_element_type=jnp.float32
        ).astype(jnp.bfloat16)
        for parity in range(2):
            pieces = []
            for j in range(chips):
                begin = (2 * j + parity) * rows
                end = min(begin + rows, width)
                pieces.append(normed[i * step : (i + 1) * step, begin:end])
                pieces.append(jnp.zeros((step, rows + 1 - (end - begin)), jnp.bfloat16))
            pieces.append(jnp.zeros((step, lanes - chips * (rows + 1)), jnp.bfloat16))
            packs[parity, i * step : (i + 1) * step, :] = jnp.concatenate(pieces, axis=1)
        at = pl.ds(i * step, step if i < PARTS - 1 else step + EXTRA)
        half = (low_ref, high_ref)[2 * i // PARTS]
        place = pl.ds(i % (PARTS // 2) * slab, slab)
        stores.append(pltpu.make_async_copy(packs.at[1 - core, at], other_ref.at[at, pl.ds(0, lanes)], left.at[3 * i + 1]))
        stores.append(pltpu.make_async_copy(product.at[i], half.at[:, place], left.at[3 * i + 2]))
        stores.append(pltpu.make_async_copy(packs.at[core, at], own_ref.at[at], left.at[3 * i + 3]))
        for store in stores[-3:]:
            store.start()
    for store in stores:
        store.wait()


def front(core, mask, inputs, upstream, weight, chips, rows):
    lanes = -(-chips * (rows + 1) // 128) * 128
    (tokens, width), columns = inputs.shape, upstream.shape[1]
    height = tokens + EXTRA
    bf16 = jnp.bfloat16
    half = jax.ShapeDtypeStruct((tokens, width // 2), bf16)
    return pl.pallas_call(
        functools.partial(front_kernel, chips, rows),
        out_shape=(
            jax.ShapeDtypeStruct((height, lanes), bf16),
            jax.ShapeDtypeStruct((height, lanes + columns), bf16),
            half,
            half,
        ),
        in_specs=[pl.BlockSpec(memory_space=pltpu.SMEM)] + [ANY] * 4,
        out_specs=(ANY,) * 4,
        scratch_shapes=[
            pltpu.VMEM(mask.shape, mask.dtype),
            pltpu.VMEM(inputs.shape, bf16),
            pltpu.VMEM((height, columns), bf16),
            pltpu.VMEM((PARTS, width // PARTS, columns), bf16),
            pltpu.VMEM((2, height, lanes), bf16),
            pltpu.VMEM((PARTS, tokens, width // PARTS), bf16),
            pltpu.SemaphoreType.DMA((2 * PARTS + 2,)),
            pltpu.SemaphoreType.DMA((3 * PARTS + 1,)),
        ],
        name="front",
        compiler_params=pltpu.CompilerParams(vmem_limit_bytes=60 << 20),
        cost_estimate=pl.CostEstimate(flops=2 * upstream.size * width, bytes_accessed=14 << 20, transcendentals=0),
    )(core, mask, inputs, upstream, weight)


def term_kernel(own_ref, other_ref, partner_ref, out_ref, own, grad, partner, first, out, arrived, left):
    lanes = own.shape[1]
    loads = [
        pltpu.make_async_copy(other_ref.at[:, pl.ds(lanes, grad.shape[1])], grad, arrived.at[0]),
        pltpu.make_async_copy(own_ref, own, arrived.at[1]),
        pltpu.make_async_copy(partner_ref, partner, arrived.at[2]),
    ]
    for load in loads:
        load.start()
    tiles = [(m, min(TILE, out.shape[0] - m)) for m in range(0, out.shape[0], TILE)]

    def product(left, right):
        return lax.dot_general(left, right, (((0,), (0,)), ((), ())), preferred_element_type=jnp.float32)

    loads[0].wait()
    loads[1].wait()
    for m, size in tiles:
        first[m : m + size, :] = product(own[:, m : m + size], grad[...])
    loads[2].wait()
    stores = []
    for i, (m, size) in enumerate(tiles):
        tile = first[m : m + size, :] + product(partner[:, m : m + size], partner[:, lanes:])
        out[m : m + size, :] = tile.astype(jnp.bfloat16)
        at = pl.ds(m, size)
        stores.append(pltpu.make_async_copy(out.at[at], out_ref.at[at], left.at[i]))
        stores[-1].start()
    for store in stores:
        store.wait()


def terms(own, other, partner, rows, width):
    return pl.pallas_call(
        term_kernel,
        out_shape=jax.ShapeDtypeStruct((rows, width), jnp.bfloat16),
        in_specs=[ANY] * 3,
        out_specs=ANY,
        scratch_shapes=[
            pltpu.VMEM(own.shape, own.dtype),
            pltpu.VMEM((own.shape[0], width), own.dtype),
            pltpu.VMEM(partner.shape, partner.dtype),
            pltpu.VMEM((rows, width), jnp.float32),
            pltpu.VMEM((rows, width), jnp.bfloat16),
            pltpu.SemaphoreType.DMA((3,)),
            pltpu.SemaphoreType.DMA((-(-rows // TILE),)),
        ],
        name="terms",
        compiler_params=pltpu.CompilerParams(vmem_limit_bytes=59 << 20),
        cost_estimate=pl.CostEstimate(flops=4 * own.shape[0] * rows * width, bytes_accessed=6 << 20, transcendentals=0),
    )(own, other, partner)


def finish_kernel(
    mine_ref, low_ref, high_ref, weight_out_ref, passed_out_ref, mine, passed, weight_out, arrived, left
):
    rows = weight_out_ref.shape[0]
    width = low_ref.shape[1]
    step = low_ref.shape[0] // (PARTS // 2)
    loads = [pltpu.make_async_copy(mine_ref, mine, arrived.at[PARTS])]
    places = []
    for i in range(PARTS):
        at, half = pl.ds(i // 2 * step, step), i % 2
        places.append((at, pl.ds(half * width, width)))
        loads.append(pltpu.make_async_copy((low_ref, high_ref)[half].at[at], passed.at[i], arrived.at[i]))
    for load in loads:
        load.start()
    loads[0].wait()
    digits = mine[rows : rows + 1, :128].astype(jnp.float32)
    lane = lax.broadcasted_iota(jnp.int32, (1, 128), 1)
    scale = jnp.where(lane < DIGITS, jnp.left_shift(1, 3 * jnp.minimum(lane, DIGITS)), 0).astype(jnp.float32)
    inverse = 1.0 / jnp.sum(digits * scale)
    for q in range(weight_out_ref.shape[1]):
        weight_out[:, q, :] = mine[:rows, 128 * q : 128 * (q + 1)].astype(jnp.float32) * inverse
    stores = [pltpu.make_async_copy(weight_out, weight_out_ref, left.at[PARTS])]
    stores[0].start()
    for i in range(PARTS):
        loads[i + 1].wait()
        passed[i] = (passed[i].astype(jnp.float32) * inverse).astype(jnp.bfloat16)
        stores.append(pltpu.make_async_copy(passed.at[i], passed_out_ref.at[places[i]], left.at[i]))
        stores[-1].start()
    for store in stores:
        store.wait()


def finish(mine, low, high):
    weight_out = jax.ShapeDtypeStruct((mine.shape[0] - 1, mine.shape[1] // 128, 128), jnp.float32)
    tokens, width = low.shape
    return pl.pallas_call(
        finish_kernel,
        out_shape=(weight_out, jax.ShapeDtypeStruct((tokens, 2 * width), low.dtype)),
        in_specs=[ANY] * 3,
        out_specs=(ANY, ANY),
        scratch_shapes=[
            pltpu.VMEM(mine.shape, mine.dtype),
            pltpu.VMEM((PARTS, tokens // (PARTS // 2), width), low.dtype),
            pltpu.VMEM(weight_out.shape, weight_out.dtype),
            pltpu.SemaphoreType.DMA((PARTS + 1,)),
            pltpu.SemaphoreType.DMA((PARTS + 1,)),
        ],
        name="finish",
        compiler_params=pltpu.CompilerParams(vmem_limit_bytes=20 << 20),
    )(mine, low, high)


def local(normed, w_value, grad_value, assistant_mask):
    inputs = normed[0]
    weight = w_value[0]
    upstream = grad_value[0]
    n = lax.axis_size("dp")
    chips = n // 2
    rows = -(-inputs.shape[1] // n)
    core = lax.rem(lax.axis_index("dp"), 2).reshape(1)

    own, other, low, high = front(core, assistant_mask[0], inputs, upstream, weight, chips, rows)
    partner = lax.ppermute(other, "dp", [(i, i ^ 1) for i in range(n)])
    low, high = (from_behind(half, "pipe", -1) for half in (low, high))
    term = terms(own, other, partner, chips * (rows + 1), upstream.shape[1])
    parity = [[2 * z + c for z in range(chips)] for c in range(2)]
    mine = lax.psum_scatter(term, "dp", scatter_dimension=0, tiled=True, axis_index_groups=parity)
    weight_grad, input_grad = finish(mine, low, high)
    return (weight_grad.reshape(1, 1, rows, -1), input_grad[None])


def solution(mesh):
    return jax.shard_map(
        local,
        mesh=mesh,
        in_specs=(
            P("pipe", "dp", "tensor"),
            P("pipe", "tensor", None),
            P("pipe", "dp", None),
            P("dp", None, None),
        ),
        out_specs=(P("pipe", "tensor", "dp", None), P("pipe", "dp", "tensor")),
        check_vma=False,
    )
```

time: 132 us -> 70 us (0.53)
  the two profiles are of different devices: /device:TPU:1 before, /device:TPU:54 now
where the time goes in v4:
time: 70 us; the launch traced here: 69.7 us
  blocking collectives  42.4 us (61%)
  Pallas kernels  13.7 us (20%)
  starting transfers between devices  10.6 us (15%)
  local copies, waits for them, and re-layouts  1.62 us (2%)
  between operations  1.4 us (2%)
    unnamed x1, blocking collectives  42.4 us
    pallas_call x1, Pallas kernels, front(): pl.pallas_call(functools.partial(front_kernel, chips, rows), out_shape=(j...  5.45 us
    ppermute x2, starting transfers between devices, from_behind(): return lax.ppermute(block, axis, route)  5.24 us
    pallas_call x1, Pallas kernels, terms(): pl.pallas_call(term_kernel, out_shape=jax.ShapeDtypeStruct((rows, width),...  5.13 us
    unnamed x1, starting transfers between devices  3.46 us
    pallas_call x1, Pallas kernels, finish(): pl.pallas_call(finish_kernel, out_shape=(weight_out, jax.ShapeDtypeStruct...  3.1 us
    ppermute x1, starting transfers between devices, local(): partner = lax.ppermute(other, 'dp', [(i, i ^ 1) for i in range(n)])  1.92 us
    unnamed x4, local copies, waits for them, and re-layouts  1.62 us
  transfers between devices with their start and end apart: 4, of which 0 were waited for; matrix products, arithmetic and copies ran while one was open for 63% of the time, Pallas kernels for 7%

profile of v4, /device:TPU:54, one launch (start us, length us, event | category | flops | bytes accessed | tf_op | source)
XLA Modules:
  0.0 69.7 jit_solution(4937235428433946628)
XLA Ops:
  0.6 5.5 %front.1 = (bf16[464,1152]{1,0:T(8,128)(2,1)}, bf16[464,2176]{1,0:T(8,128)(2,1)}, bf16[448,1024]{1,0:T(8,128)(2,1)}, bf16[448,1024]{1,0:T(8,128)(2,1)}) custom-call(s32[1]{0:T(128)} %bitcast.core_ref, s32[4,8192]{1,0:T(4,128)} %bitcast.13, bf16[448,2048]{1,0:T(8,128)(2,1)} %bitcast.11, bf16[448,1024]{1,0:T(8,128)(2,1)} %bitcast.12, bf16[2048,1024]{1,0:T(8,128)(2,1)} %bitcast.10), custom_call_target="tpu_custom_call" | custom-call | flops 1879048192 | bytes 14680064 | tf_op jit(solution)/shard_map/front/pallas_call | solution.py:93
  6.1 1.9 %collective-permute-start = (bf16[464,2176]{1,0:T(8,128)(2,1)}, bf16[464,2176]{1,0:T(8,128)(2,1)}, u32[]{:S(2)}, u32[]{:S(2)}) collective-permute-start(bf16[464,2176]{1,0:T(8,128)(2,1)} %get-tuple-element.9.other_ref), channel_id=1, source_target_pairs={{0,32},{32,0},{64,96},{96,64},{128,160},{160,128},{192,224},{224,1... | collective-permute-start | bytes 6057992 | tf_op jit(solution)/shard_map/ppermute | solution.py:232
  8.0 2.8 %collective-permute-start.1 = (bf16[448,1024]{1,0:T(8,128)(2,1)}, bf16[448,1024]{1,0:T(8,128)(2,1)S(1)}, u32[]{:S(2)}, u32[]{:S(2)}) collective-permute-start(bf16[448,1024]{1,0:T(8,128)(2,1)} %get-tuple-element.10), channel_id=1, source_target_pairs={{1,0},{2,1},{3,2},{5,4},{6,5},{7,6},{9,8},{10,9},{11,10},{13,12},{... | collective-permute-start | bytes 2752520 | tf_op jit(solution)/shard_map/ppermute | solution.py:21
  10.8 2.4 %collective-permute-start.2 = (bf16[448,1024]{1,0:T(8,128)(2,1)}, bf16[448,1024]{1,0:T(8,128)(2,1)S(1)}, u32[]{:S(2)}, u32[]{:S(2)}) collective-permute-start(bf16[448,1024]{1,0:T(8,128)(2,1)} %get-tuple-element.11), channel_id=1, source_target_pairs={{1,0},{2,1},{3,2},{5,4},{6,5},{7,6},{9,8},{10,9},{11,10},{13,12},{... | collective-permute-start | bytes 2752520 | tf_op jit(solution)/shard_map/ppermute | solution.py:21
  13.3 0.0 collective-permute-done.partner_ref
  13.3 5.1 %terms.1 = bf16[1044,1024]{1,0:T(8,128)(2,1)} custom-call(bf16[464,1152]{1,0:T(8,128)(2,1)} %get-tuple-element.8.own_ref, bf16[464,2176]{1,0:T(8,128)(2,1)} %get-tuple-element.9.other_ref, bf16[464,2176]{1,0:T(8,128)(2,1)} %collective-permute-done.partner_ref), custom_call_target="tpu_custom_call" | custom-call | flops 1984167936 | bytes 6291456 | tf_op jit(solution)/shard_map/terms/pallas_call | solution.py:150
  18.4 42.4 %fusion = bf16[88,1024]{1,0:T(8,128)(2,1)S(1)} fusion(bf16[1044,1024]{1,0:T(8,128)(2,1)} %terms.1), kind=kCustom, calls=%all-reduce-scatter | all-reduce-scatter fusion | flops 1081345 | bytes 2322432
  60.8 3.5 %collective-permute-start.3 = (bf16[11,1024]{1,0:T(8,128)(2,1)S(1)}, bf16[11,1024]{1,0:T(8,128)(2,1)S(1)}, u32[]{:S(2)}, u32[]{:S(2)}) collective-permute-start(bf16[11,1024]{1,0:T(8,128)(2,1)S(1)} %slice), channel_id=1, source_target_pairs={{0,64},{64,128},{128,192},{192,256},{256,320},{320,384},{384,448},... | collective-permute-start | bytes 67592
  64.3 1.3 %dynamic-slice.4 = u32[1]{0:T(128)} dynamic-slice(u32[768]{0:T(1024)} %constant.16, u32[]{:S(6)} %partition-id.4), dynamic_slice_sizes={1} | dynamic-slice | bytes 12
  66.2 0.0 collective-permute-done.3
  66.3 0.3 concatenate
  66.5 0.1 constant_dynamic-slice_fusion.mine_ref
  66.6 0.0 collective-permute-done.1.low_ref
  66.6 0.0 collective-permute-done.2.high_ref
  66.6 3.1 %finish.1 = (f32[86,8,128]{2,1,0:T(8,128)}, bf16[448,2048]{1,0:T(8,128)(2,1)}) custom-call(bf16[87,1024]{1,0:T(8,128)(2,1)S(1)} %constant_dynamic-slice_fusion.mine_ref, bf16[448,1024]{1,0:T(8,128)(2,1)S(1)} %collective-permute-done.1.low_ref, bf16[448,1024]{1,0:T(8,128)(2,1)S(1)} %collective-permute-done.2.high_ref), custom_call_target="tpu_custom_call" | custom-call | tf_op jit(solution)/shard_map/finish/pallas_call | solution.py:205
  (1 shorter events, 0.0 us)
Async XLA Ops:
  6.1 7.2 %collective-permute-start = (bf16[464,2176]{1,0:T(8,128)(2,1)}, bf16[464,2176]{1,0:T(8,128)(2,1)}, u32[]{:S(2)}, u32[]{:S(2)}) collective-permute-start(bf16[464,2176]{1,0:T(8,128)(2,1)} %get-tuple-element.9.other_ref), channel_id=1, source_target_pairs={{0,32},{32,0},{64,96},{96,64},{128,160},{160,128},{192,224},{224,1... | collective-permute-start | bytes 6057992 | tf_op jit(solution)/shard_map/ppermute | solution.py:232
  8.0 58.6 %collective-permute-start.1 = (bf16[448,1024]{1,0:T(8,128)(2,1)}, bf16[448,1024]{1,0:T(8,128)(2,1)S(1)}, u32[]{:S(2)}, u32[]{:S(2)}) collective-permute-start(bf16[448,1024]{1,0:T(8,128)(2,1)} %get-tuple-element.10), channel_id=1, source_target_pairs={{1,0},{2,1},{3,2},{5,4},{6,5},{7,6},{9,8},{10,9},{11,10},{13,12},{... | collective-permute-start | bytes 2752520 | tf_op jit(solution)/shard_map/ppermute | solution.py:21
  10.8 55.8 %collective-permute-start.2 = (bf16[448,1024]{1,0:T(8,128)(2,1)}, bf16[448,1024]{1,0:T(8,128)(2,1)S(1)}, u32[]{:S(2)}, u32[]{:S(2)}) collective-permute-start(bf16[448,1024]{1,0:T(8,128)(2,1)} %get-tuple-element.11), channel_id=1, source_target_pairs={{1,0},{2,1},{3,2},{5,4},{6,5},{7,6},{9,8},{10,9},{11,10},{13,12},{... | collective-permute-start | bytes 2752520 | tf_op jit(solution)/shard_map/ppermute | solution.py:21
  60.8 5.4 %collective-permute-start.3 = (bf16[11,1024]{1,0:T(8,128)(2,1)S(1)}, bf16[11,1024]{1,0:T(8,128)(2,1)S(1)}, u32[]{:S(2)}, u32[]{:S(2)}) collective-permute-start(bf16[11,1024]{1,0:T(8,128)(2,1)S(1)} %slice), channel_id=1, source_target_pairs={{0,64},{64,128},{128,192},{192,256},{256,320},{320,384},{384,448},... | collective-permute-start | bytes 67592

commit v5 on v4

v5 whole, which is shorter than its diff:
```python
import functools

import jax
import jax.numpy as jnp
from jax import lax
from jax.experimental import pallas as pl
from jax.experimental.pallas import tpu as pltpu
from jax.sharding import PartitionSpec as P

DIGITS = 6
EXTRA = 16
FRONT = 60_000_000
TILE = 256
PARTS = 4
VM = pl.BlockSpec(memory_space=pltpu.VMEM)
ANY = pl.BlockSpec(memory_space=pl.ANY)


def from_behind(block, axis, distance):
    devices = range(lax.axis_size(axis))
    route = [(i - distance, i) for i in devices if i - distance in devices]
    return lax.ppermute(block, axis, route)


def front_kernel(
    chips, rows, core_ref, mask_ref, normed_ref, grad_ref, weight_ref, own_ref, own_grad_ref, other_ref, low_ref, high_ref,
    mask, normed, grad, weight, packs, made, arrived, left,
):
    tokens, width = normed.shape
    lanes, columns = own_ref.shape[1], grad_ref.shape[1]
    step, slab = tokens // PARTS, width // PARTS
    loads = [
        pltpu.make_async_copy(grad_ref, grad.at[pl.ds(0, tokens)], arrived.at[0]),
        pltpu.make_async_copy(mask_ref, mask, arrived.at[1]),
    ]
    for i in range(PARTS):
        at = pl.ds(i * step, step)
        loads.append(pltpu.make_async_copy(weight_ref.at[pl.ds(i * slab, slab)], weight.at[i], arrived.at[2 * i + 2]))
        loads.append(pltpu.make_async_copy(normed_ref.at[at], normed.at[at], arrived.at[2 * i + 3]))
    for load in loads:
        load.start()

    at = lax.broadcasted_iota(jnp.int32, (EXTRA, lanes), 1)
    first = lax.broadcasted_iota(jnp.int32, (EXTRA, lanes), 0) == 0
    marks = first & (at % (rows + 1) == rows) & (at < chips * (rows + 1))
    marks = jnp.where(marks, 1.0, 0.0).astype(jnp.bfloat16)
    for parity in range(2):
        packs[parity, tokens:, :] = marks
    lane = lax.broadcasted_iota(jnp.int32, (EXTRA, columns), 1)
    row = lax.broadcasted_iota(jnp.int32, (EXTRA, columns), 0)
    loads[0].wait()
    loads[1].wait()
    count = jnp.sum(mask[...])
    digit = jnp.bitwise_and(jnp.right_shift(count, 3 * jnp.minimum(lane, DIGITS)), 7)
    digit = jnp.where((lane < DIGITS) & (row == 0), digit, 0).astype(jnp.float32).astype(jnp.bfloat16)
    grad[tokens:, :] = digit
    core = core_ref[0]
    stores = [
        pltpu.make_async_copy(grad, other_ref.at[:, pl.ds(lanes, columns)], left.at[0]),
        pltpu.make_async_copy(grad, own_grad_ref, left.at[3 * PARTS + 1]),
    ]
    for store in stores:
        store.start()

    for i in range(PARTS):
        loads[2 * i + 2].wait()
        loads[2 * i + 3].wait()
        made[i] = lax.dot_general(
            grad[:tokens, :], weight[i], (((1,), (1,)), ((), ())), preferred_element_type=jnp.float32
        ).astype(jnp.bfloat16)
        for parity in range(2):
            pieces = []
            for j in range(chips):
                begin = (2 * j + parity) * rows
                end = min(begin + rows, width)
                pieces.append(normed[i * step : (i + 1) * step, begin:end])
                pieces.append(jnp.zeros((step, rows + 1 - (end - begin)), jnp.bfloat16))
            pieces.append(jnp.zeros((step, lanes - chips * (rows + 1)), jnp.bfloat16))
            packs[parity, i * step : (i + 1) * step, :] = jnp.concatenate(pieces, axis=1)
        at = pl.ds(i * step, step if i < PARTS - 1 else step + EXTRA)
        half = (low_ref, high_ref)[2 * i // PARTS]
        place = pl.ds(i % (PARTS // 2) * slab, slab)
        stores.append(pltpu.make_async_copy(packs.at[1 - core, at], other_ref.at[at, pl.ds(0, lanes)], left.at[3 * i + 1]))
        stores.append(pltpu.make_async_copy(made.at[i], half.at[:, place], left.at[3 * i + 2]))
        stores.append(pltpu.make_async_copy(packs.at[core, at], own_ref.at[at], left.at[3 * i + 3]))
        for store in stores[-3:]:
            store.start()
    for store in stores:
        store.wait()


def front(core, mask, inputs, upstream, weight, chips, rows):
    lanes = -(-chips * (rows + 1) // 128) * 128
    (tokens, width), columns = inputs.shape, upstream.shape[1]
    height = tokens + EXTRA
    bf16 = jnp.bfloat16
    half = jax.ShapeDtypeStruct((tokens, width // 2), bf16)
    return pl.pallas_call(
        functools.partial(front_kernel, chips, rows),
        out_shape=(
            jax.ShapeDtypeStruct((height, lanes), bf16),
            jax.ShapeDtypeStruct((height, columns), bf16),
            jax.ShapeDtypeStruct((height, lanes + columns), bf16),
            half,
            half,
        ),
        in_specs=[pl.BlockSpec(memory_space=pltpu.SMEM)] + [ANY] * 4,
        out_specs=(ANY,) * 5,
        scratch_shapes=[
            pltpu.VMEM(mask.shape, mask.dtype),
            pltpu.VMEM(inputs.shape, bf16),
            pltpu.VMEM((height, columns), bf16),
            pltpu.VMEM((PARTS, width // PARTS, columns), bf16),
            pltpu.VMEM((2, height, lanes), bf16),
            pltpu.VMEM((PARTS, tokens, width // PARTS), bf16),
            pltpu.SemaphoreType.DMA((2 * PARTS + 2,)),
            pltpu.SemaphoreType.DMA((3 * PARTS + 2,)),
        ],
        name="front",
        compiler_params=pltpu.CompilerParams(vmem_limit_bytes=FRONT),
        cost_estimate=pl.CostEstimate(flops=2 * upstream.size * width, bytes_accessed=14 << 20, transcendentals=0),
    )(core, mask, inputs, upstream, weight)


def product(left, right):
    return lax.dot_general(left, right, (((0,), (0,)), ((), ())), preferred_element_type=jnp.float32)


def own_kernel(own_ref, grad_ref, out_ref):
    for m in range(0, out_ref.shape[0], TILE):
        size = min(TILE, out_ref.shape[0] - m)
        out_ref[m : m + size, :] = product(own_ref[:, m : m + size], grad_ref[...])


def own_terms(own, grad, rows):
    width = grad.shape[1]
    return pl.pallas_call(
        own_kernel,
        out_shape=jax.ShapeDtypeStruct((rows, width), jnp.float32),
        in_specs=[VM] * 2,
        out_specs=VM,
        name="own_terms",
        compiler_params=pltpu.CompilerParams(vmem_limit_bytes=20 << 20),
        cost_estimate=pl.CostEstimate(flops=2 * own.shape[0] * rows * width, bytes_accessed=6 << 20, transcendentals=0),
    )(own, grad)


def term_kernel(partner_ref, first_ref, out_ref):
    lanes = partner_ref.shape[1] - out_ref.shape[1]
    for m in range(0, out_ref.shape[0], TILE):
        size = min(TILE, out_ref.shape[0] - m)
        tile = product(partner_ref[:, m : m + size], partner_ref[:, lanes:]) + first_ref[m : m + size, :]
        out_ref[m : m + size, :] = tile.astype(out_ref.dtype)


def terms(partner, first):
    rows, width = first.shape
    return pl.pallas_call(
        term_kernel,
        out_shape=jax.ShapeDtypeStruct((rows, width), jnp.bfloat16),
        in_specs=[VM] * 2,
        out_specs=VM,
        name="terms",
        compiler_params=pltpu.CompilerParams(vmem_limit_bytes=20 << 20),
        cost_estimate=pl.CostEstimate(
            flops=2 * partner.shape[0] * rows * width, bytes_accessed=8 << 20, transcendentals=0
        ),
    )(partner, first)


def finish_kernel(mine_ref, low_ref, high_ref, weight_out_ref, passed_out_ref, passed, weight_out, left):
    rows = weight_out_ref.shape[0]
    width = low_ref.shape[1]
    step = low_ref.shape[0] // (PARTS // 2)
    digits = mine_ref[rows : rows + 1, :128].astype(jnp.float32)
    lane = lax.broadcasted_iota(jnp.int32, (1, 128), 1)
    scale = jnp.where(lane < DIGITS, jnp.left_shift(1, 3 * jnp.minimum(lane, DIGITS)), 0).astype(jnp.float32)
    inverse = 1.0 / jnp.sum(digits * scale)
    stores = []
    for i in range(PARTS):
        low, half = i // 2 * step, i % 2
        passed[i] = ((low_ref, high_ref)[half][low : low + step, :].astype(jnp.float32) * inverse).astype(jnp.bfloat16)
        place = passed_out_ref.at[pl.ds(low, step), pl.ds(half * width, width)]
        stores.append(pltpu.make_async_copy(passed.at[i], place, left.at[i]))
        stores[-1].start()
    for q in range(weight_out_ref.shape[1]):
        weight_out[:, q, :] = mine_ref[:rows, 128 * q : 128 * (q + 1)].astype(jnp.float32) * inverse
    stores.append(pltpu.make_async_copy(weight_out, weight_out_ref, left.at[PARTS]))
    stores[-1].start()
    for store in stores:
        store.wait()


def finish(mine, low, high):
    weight_out = jax.ShapeDtypeStruct((mine.shape[0] - 1, mine.shape[1] // 128, 128), jnp.float32)
    tokens, width = low.shape
    return pl.pallas_call(
        finish_kernel,
        out_shape=(weight_out, jax.ShapeDtypeStruct((tokens, 2 * width), low.dtype)),
        in_specs=[VM] * 3,
        out_specs=(ANY, ANY),
        scratch_shapes=[
            pltpu.VMEM((PARTS, tokens // (PARTS // 2), width), low.dtype),
            pltpu.VMEM(weight_out.shape, weight_out.dtype),
            pltpu.SemaphoreType.DMA((PARTS + 1,)),
        ],
        name="finish",
        compiler_params=pltpu.CompilerParams(vmem_limit_bytes=20 << 20),
    )(mine, low, high)


def local(normed, w_value, grad_value, assistant_mask):
    inputs = normed[0]
    weight = w_value[0]
    upstream = grad_value[0]
    n = lax.axis_size("dp")
    chips = n // 2
    rows = -(-inputs.shape[1] // n)
    core = lax.rem(lax.axis_index("dp"), 2).reshape(1)

    own, grad, other, low, high = front(core, assistant_mask[0], inputs, upstream, weight, chips, rows)
    partner = lax.ppermute(other, "dp", [(i, i ^ 1) for i in range(n)])
    low, high = (from_behind(half, "pipe", -1) for half in (low, high))
    term = terms(partner, own_terms(own, grad, chips * (rows + 1)))
    parity = [[2 * z + c for z in range(chips)] for c in range(2)]
    mine = lax.psum_scatter(term, "dp", scatter_dimension=0, tiled=True, axis_index_groups=parity)
    weight_grad, input_grad = finish(mine, low, high)
    return (weight_grad.reshape(1, 1, rows, -1), input_grad[None])


def solution(mesh):
    return jax.shard_map(
        local,
        mesh=mesh,
        in_specs=(
            P("pipe", "dp", "tensor"),
            P("pipe", "tensor", None),
            P("pipe", "dp", None),
            P("dp", None, None),
        ),
        out_specs=(P("pipe", "tensor", "dp", None), P("pipe", "dp", "tensor")),
        check_vma=False,
    )
```

time: 70 us -> 70.9 us (1.013)
  the two profiles are of different devices: /device:TPU:54 before, /device:TPU:38 now
where the time goes in v5:
time: 70.9 us; the launch traced here: 70.5 us
  blocking collectives  41.8 us (59%)
  Pallas kernels  11.8 us (17%)
  starting transfers between devices  11.5 us (16%)
  local copies, waits for them, and re-layouts  4.04 us (6%)
  between operations  1.38 us (2%)
    unnamed x1, blocking collectives  41.8 us
    ppermute x2, starting transfers between devices, from_behind(): return lax.ppermute(block, axis, route)  6.16 us
    pallas_call x1, Pallas kernels, front(): pl.pallas_call(functools.partial(front_kernel, chips, rows), out_shape=(j...  6.15 us
    unnamed x8, local copies, waits for them, and re-layouts  4.04 us
    unnamed x1, starting transfers between devices  3.46 us
    pallas_call x1, Pallas kernels, finish(): pl.pallas_call(finish_kernel, out_shape=(weight_out, jax.ShapeDtypeStruct...  2.85 us
    ppermute x1, starting transfers between devices, local(): partner = lax.ppermute(other, 'dp', [(i, i ^ 1) for i in range(n)])  1.92 us
    pallas_call x1, Pallas kernels, terms(): pl.pallas_call(term_kernel, out_shape=jax.ShapeDtypeStruct((rows, width),...  1.42 us
  transfers between devices with their start and end apart: 4, of which 0 were waited for; matrix products, arithmetic and copies ran while one was open for 62% of the time, Pallas kernels for 4%

profile of v5, /device:TPU:38, one launch (start us, length us, event | category | flops | bytes accessed | tf_op | source)
XLA Modules:
  0.0 70.5 jit_solution(812009848046104186)
XLA Ops:
  0.6 6.2 %front.1 = (bf16[464,1152]{1,0:T(8,128)(2,1)}, bf16[464,1024]{1,0:T(8,128)(2,1)}, bf16[464,2176]{1,0:T(8,128)(2,1)}, bf16[448,1024]{1,0:T(8,128)(2,1)}, bf16[448,1024]{1,0:T(8,128)(2,1)}) custom-call(s32[1]{0:T(128)} %bitcast.core_ref, s32[4,8192]{1,0:T(4,128)} %bitcast.13, bf16[448,2048]{1,0:T(8,128)(2,1)} %bitcast.11, bf16[448,1024]{1,0:T(8,128)(2,1)} %bitcast.12, ...), custom_call_target="tpu_custom_call" | custom-call | flops 1879048192 | bytes 14680064 | tf_op jit(solution)/shard_map/front/pallas_call | solution.py:98
  6.8 1.9 %collective-permute-start = (bf16[464,2176]{1,0:T(8,128)(2,1)}, bf16[464,2176]{1,0:T(8,128)(2,1)S(1)}, u32[]{:S(2)}, u32[]{:S(2)}) collective-permute-start(bf16[464,2176]{1,0:T(8,128)(2,1)} %get-tuple-element.9), channel_id=1, source_target_pairs={{0,32},{32,0},{64,96},{96,64},{128,160},{160,128},{192,224},{224,1... | collective-permute-start | bytes 6057992 | tf_op jit(solution)/shard_map/ppermute | solution.py:222
  8.7 2.8 %collective-permute-start.1 = (bf16[448,1024]{1,0:T(8,128)(2,1)}, bf16[448,1024]{1,0:T(8,128)(2,1)S(1)}, u32[]{:S(2)}, u32[]{:S(2)}) collective-permute-start(bf16[448,1024]{1,0:T(8,128)(2,1)} %get-tuple-element.12), channel_id=1, source_target_pairs={{1,0},{2,1},{3,2},{5,4},{6,5},{7,6},{9,8},{10,9},{11,10},{13,12},{... | collective-permute-start | bytes 2752520 | tf_op jit(solution)/shard_map/ppermute | solution.py:22
  11.5 3.4 %collective-permute-start.2 = (bf16[448,1024]{1,0:T(8,128)(2,1)}, bf16[448,1024]{1,0:T(8,128)(2,1)}, u32[]{:S(2)}, u32[]{:S(2)}) collective-permute-start(bf16[448,1024]{1,0:T(8,128)(2,1)} %get-tuple-element.13), channel_id=1, source_target_pairs={{1,0},{2,1},{3,2},{5,4},{6,5},{7,6},{9,8},{10,9},{11,10},{13,12},{... | collective-permute-start | bytes 2752520 | tf_op jit(solution)/shard_map/ppermute | solution.py:22
  14.9 0.0 copy-start
  14.9 1.2 %copy-done = bf16[464,1152]{1,0:T(8,128)(2,1)S(1)} copy-done((bf16[464,1152]{1,0:T(8,128)(2,1)S(1)}, bf16[464,1152]{1,0:T(8,128)(2,1)}, u32[]{:S(2)}) %copy-start) | copy-done | bytes 1069080
  16.1 0.0 copy-start.1
  16.1 1.2 %copy-done.1 = bf16[464,1024]{1,0:T(8,128)(2,1)S(1)} copy-done((bf16[464,1024]{1,0:T(8,128)(2,1)S(1)}, bf16[464,1024]{1,0:T(8,128)(2,1)}, u32[]{:S(2)}) %copy-start.1) | copy-done | bytes 950296
  17.3 1.4 %own_terms.1.first_ref = f32[1044,1024]{1,0:T(8,128)S(1)} custom-call(bf16[464,1152]{1,0:T(8,128)(2,1)S(1)} %copy-done, bf16[464,1024]{1,0:T(8,128)(2,1)S(1)} %copy-done.1), custom_call_target="tpu_custom_call" | custom-call | flops 992083968 | bytes 6291456 | tf_op jit(solution)/shard_map/own_terms/pallas_call | solution.py:137
  18.7 0.0 collective-permute-done.partner_ref
  18.7 1.4 %terms.1 = bf16[1044,1024]{1,0:T(8,128)(2,1)S(1)} custom-call(bf16[464,2176]{1,0:T(8,128)(2,1)S(1)} %collective-permute-done.partner_ref, f32[1044,1024]{1,0:T(8,128)S(1)} %own_terms.1.first_ref), custom_call_target="tpu_custom_call" | custom-call | flops 992083968 | bytes 8388608 | tf_op jit(solution)/shard_map/terms/pallas_call | solution.py:158
  20.1 41.8 %fusion = bf16[88,1024]{1,0:T(8,128)(2,1)S(1)} fusion(bf16[1044,1024]{1,0:T(8,128)(2,1)S(1)} %terms.1), kind=kCustom, calls=%all-reduce-scatter | all-reduce-scatter fusion | flops 1081345 | bytes 2322432
  61.9 3.5 %collective-permute-start.3 = (bf16[11,1024]{1,0:T(8,128)(2,1)S(1)}, bf16[11,1024]{1,0:T(8,128)(2,1)S(1)}, u32[]{:S(2)}, u32[]{:S(2)}) collective-permute-start(bf16[11,1024]{1,0:T(8,128)(2,1)S(1)} %slice), channel_id=1, source_target_pairs={{0,64},{64,128},{128,192},{192,256},{256,320},{320,384},{384,448},... | collective-permute-start | bytes 67592
  65.4 1.3 %dynamic-slice.4 = u32[1]{0:T(128)} dynamic-slice(u32[768]{0:T(1024)} %constant.16, u32[]{:S(6)} %partition-id.4), dynamic_slice_sizes={1} | dynamic-slice | bytes 12
  67.3 0.0 collective-permute-done.3
  67.3 0.3 concatenate
  67.6 0.1 constant_dynamic-slice_fusion.mine_ref
  67.7 0.0 collective-permute-done.1.low_ref
  67.7 0.0 collective-permute-done.2.high_ref
  67.7 2.8 %finish.1 = (f32[86,8,128]{2,1,0:T(8,128)}, bf16[448,2048]{1,0:T(8,128)(2,1)}) custom-call(bf16[87,1024]{1,0:T(8,128)(2,1)S(1)} %constant_dynamic-slice_fusion.mine_ref, bf16[448,1024]{1,0:T(8,128)(2,1)S(1)} %collective-permute-done.1.low_ref, bf16[448,1024]{1,0:T(8,128)(2,1)} %collective-permute-done.2.high_ref), custom_call_target="tpu_custom_call" | custom-call | tf_op jit(solution)/shard_map/finish/pallas_call | solution.py:197
  (1 shorter events, 0.0 us)
Async XLA Ops:
  6.8 11.9 %collective-permute-start = (bf16[464,2176]{1,0:T(8,128)(2,1)}, bf16[464,2176]{1,0:T(8,128)(2,1)S(1)}, u32[]{:S(2)}, u32[]{:S(2)}) collective-permute-start(bf16[464,2176]{1,0:T(8,128)(2,1)} %get-tuple-element.9), channel_id=1, source_target_pairs={{0,32},{32,0},{64,96},{96,64},{128,160},{160,128},{192,224},{224,1... | collective-permute-start | bytes 6057992 | tf_op jit(solution)/shard_map/ppermute | solution.py:222
  8.7 59.0 %collective-permute-start.1 = (bf16[448,1024]{1,0:T(8,128)(2,1)}, bf16[448,1024]{1,0:T(8,128)(2,1)S(1)}, u32[]{:S(2)}, u32[]{:S(2)}) collective-permute-start(bf16[448,1024]{1,0:T(8,128)(2,1)} %get-tuple-element.12), channel_id=1, source_target_pairs={{1,0},{2,1},{3,2},{5,4},{6,5},{7,6},{9,8},{10,9},{11,10},{13,12},{... | collective-permute-start | bytes 2752520 | tf_op jit(solution)/shard_map/ppermute | solution.py:22
  11.5 56.2 %collective-permute-start.2 = (bf16[448,1024]{1,0:T(8,128)(2,1)}, bf16[448,1024]{1,0:T(8,128)(2,1)}, u32[]{:S(2)}, u32[]{:S(2)}) collective-permute-start(bf16[448,1024]{1,0:T(8,128)(2,1)} %get-tuple-element.13), channel_id=1, source_target_pairs={{1,0},{2,1},{3,2},{5,4},{6,5},{7,6},{9,8},{10,9},{11,10},{13,12},{... | collective-permute-start | bytes 2752520 | tf_op jit(solution)/shard_map/ppermute | solution.py:22
  14.9 1.2 %copy-start = (bf16[464,1152]{1,0:T(8,128)(2,1)S(1)}, bf16[464,1152]{1,0:T(8,128)(2,1)}, u32[]{:S(2)}) copy-start(bf16[464,1152]{1,0:T(8,128)(2,1)} %get-tuple-element.10.own_ref) | copy-start | bytes 3207172
  16.1 1.2 %copy-start.1 = (bf16[464,1024]{1,0:T(8,128)(2,1)S(1)}, bf16[464,1024]{1,0:T(8,128)(2,1)}, u32[]{:S(2)}) copy-start(bf16[464,1024]{1,0:T(8,128)(2,1)} %get-tuple-element.11.grad_ref) | copy-start | bytes 2850820
  61.9 5.4 %collective-permute-start.3 = (bf16[11,1024]{1,0:T(8,128)(2,1)S(1)}, bf16[11,1024]{1,0:T(8,128)(2,1)S(1)}, u32[]{:S(2)}, u32[]{:S(2)}) collective-permute-start(bf16[11,1024]{1,0:T(8,128)(2,1)S(1)} %slice), channel_id=1, source_target_pairs={{0,64},{64,128},{128,192},{192,256},{256,320},{320,384},{384,448},... | collective-permute-start | bytes 67592

commit v6 on v5

--- a/solution.py
+++ b/solution.py
@@ -9,7 +9,6 @@
 
 DIGITS = 6
 EXTRA = 16
-FRONT = 60_000_000
 TILE = 256
 PARTS = 4
 VM = pl.BlockSpec(memory_space=pltpu.VMEM)
@@ -23,8 +22,8 @@
 
 
 def front_kernel(
-    chips, rows, core_ref, mask_ref, normed_ref, grad_ref, weight_ref, own_ref, own_grad_ref, other_ref, low_ref, high_ref,
-    mask, normed, grad, weight, packs, made, arrived, left,
+    chips, rows, core_ref, mask_ref, normed_ref, grad_ref, weight_ref, own_ref, grad, other_ref, low_ref, high_ref,
+    mask, normed, weight, packs, made, arrived, left,
 ):
     tokens, width = normed.shape
     lanes, columns = own_ref.shape[1], grad_ref.shape[1]
@@ -55,12 +54,8 @@
     digit = jnp.where((lane < DIGITS) & (row == 0), digit, 0).astype(jnp.float32).astype(jnp.bfloat16)
     grad[tokens:, :] = digit
     core = core_ref[0]
-    stores = [
-        pltpu.make_async_copy(grad, other_ref.at[:, pl.ds(lanes, columns)], left.at[0]),
-        pltpu.make_async_copy(grad, own_grad_ref, left.at[3 * PARTS + 1]),
-    ]
-    for store in stores:
-        store.start()
+    stores = [pltpu.make_async_copy(grad, other_ref.at[:, pl.ds(lanes, columns)], left.at[0])]
+    stores[0].start()
 
     for i in range(PARTS):
         loads[2 * i + 2].wait()
@@ -80,8 +75,8 @@
         at = pl.ds(i * step, step if i < PARTS - 1 else step + EXTRA)
         half = (low_ref, high_ref)[2 * i // PARTS]
         place = pl.ds(i % (PARTS // 2) * slab, slab)
-        stores.append(pltpu.make_async_copy(packs.at[1 - core, at], other_ref.at[at, pl.ds(0, lanes)], left.at[3 * i + 1]))
-        stores.append(pltpu.make_async_copy(made.at[i], half.at[:, place], left.at[3 * i + 2]))
+        stores.append(pltpu.make_async_copy(made.at[i], half.at[:, place], left.at[3 * i + 1]))
+        stores.append(pltpu.make_async_copy(packs.at[1 - core, at], other_ref.at[at, pl.ds(0, lanes)], left.at[3 * i + 2]))
         stores.append(pltpu.make_async_copy(packs.at[core, at], own_ref.at[at], left.at[3 * i + 3]))
         for store in stores[-3:]:
             store.start()
@@ -94,30 +89,29 @@
     (tokens, width), columns = inputs.shape, upstream.shape[1]
     height = tokens + EXTRA
     bf16 = jnp.bfloat16
-    half = jax.ShapeDtypeStruct((tokens, width // 2), bf16)
+    half = pltpu.HBM((tokens, width // 2), bf16)
     return pl.pallas_call(
         functools.partial(front_kernel, chips, rows),
         out_shape=(
-            jax.ShapeDtypeStruct((height, lanes), bf16),
-            jax.ShapeDtypeStruct((height, columns), bf16),
-            jax.ShapeDtypeStruct((height, lanes + columns), bf16),
+            pltpu.VMEM((height, lanes), bf16),
+            pltpu.VMEM((height, columns), bf16),
+            pltpu.VMEM((height, lanes + columns), bf16),
             half,
             half,
         ),
-        in_specs=[pl.BlockSpec(memory_space=pltpu.SMEM)] + [ANY] * 4,
-        out_specs=(ANY,) * 5,
+        in_specs=[pl.BlockSpec(memory_space=pltpu.SMEM)] + [pl.BlockSpec(memory_space=pltpu.HBM)] * 4,
+        out_specs=(VM,) * 3 + (pl.BlockSpec(memory_space=pltpu.HBM),) * 2,
         scratch_shapes=[
             pltpu.VMEM(mask.shape, mask.dtype),
             pltpu.VMEM(inputs.shape, bf16),
-            pltpu.VMEM((height, columns), bf16),
             pltpu.VMEM((PARTS, width // PARTS, columns), bf16),
             pltpu.VMEM((2, height, lanes), bf16),
             pltpu.VMEM((PARTS, tokens, width // PARTS), bf16),
             pltpu.SemaphoreType.DMA((2 * PARTS + 2,)),
-            pltpu.SemaphoreType.DMA((3 * PARTS + 2,)),
+            pltpu.SemaphoreType.DMA((3 * PARTS + 1,)),
         ],
         name="front",
-        compiler_params=pltpu.CompilerParams(vmem_limit_bytes=FRONT),
+        compiler_params=pltpu.CompilerParams(vmem_limit_bytes=40 << 20),
         cost_estimate=pl.CostEstimate(flops=2 * upstream.size * width, bytes_accessed=14 << 20, transcendentals=0),
     )(core, mask, inputs, upstream, weight)
 
@@ -168,18 +162,25 @@
     )(partner, first)
 
 
-def finish_kernel(mine_ref, low_ref, high_ref, weight_out_ref, passed_out_ref, passed, weight_out, left):
+def finish_kernel(
+    mine_ref, low_ref, high_ref, weight_out_ref, passed_out_ref, high, passed, weight_out, arrived, left
+):
     rows = weight_out_ref.shape[0]
     width = low_ref.shape[1]
     step = low_ref.shape[0] // (PARTS // 2)
+    load = pltpu.make_async_copy(high_ref, high, arrived)
+    load.start()
     digits = mine_ref[rows : rows + 1, :128].astype(jnp.float32)
     lane = lax.broadcasted_iota(jnp.int32, (1, 128), 1)
     scale = jnp.where(lane < DIGITS, jnp.left_shift(1, 3 * jnp.minimum(lane, DIGITS)), 0).astype(jnp.float32)
     inverse = 1.0 / jnp.sum(digits * scale)
     stores = []
     for i in range(PARTS):
-        low, half = i // 2 * step, i % 2
-        passed[i] = ((low_ref, high_ref)[half][low : low + step, :].astype(jnp.float32) * inverse).astype(jnp.bfloat16)
+        half, low = divmod(i, PARTS // 2)
+        low *= step
+        if half and not low:
+            load.wait()
+        passed[i] = ((low_ref, high)[half][low : low + step, :].astype(jnp.float32) * inverse).astype(jnp.bfloat16)
         place = passed_out_ref.at[pl.ds(low, step), pl.ds(half * width, width)]
         stores.append(pltpu.make_async_copy(passed.at[i], place, left.at[i]))
         stores[-1].start()
@@ -197,11 +198,13 @@
     return pl.pallas_call(
         finish_kernel,
         out_shape=(weight_out, jax.ShapeDtypeStruct((tokens, 2 * width), low.dtype)),
-        in_specs=[VM] * 3,
+        in_specs=[VM, VM, ANY],
         out_specs=(ANY, ANY),
         scratch_shapes=[
+            pltpu.VMEM(high.shape, high.dtype),
             pltpu.VMEM((PARTS, tokens // (PARTS // 2), width), low.dtype),
             pltpu.VMEM(weight_out.shape, weight_out.dtype),
+            pltpu.SemaphoreType.DMA,
             pltpu.SemaphoreType.DMA((PARTS + 1,)),
         ],
         name="finish",
@@ -218,7 +221,8 @@
     rows = -(-inputs.shape[1] // n)
     core = lax.rem(lax.axis_index("dp"), 2).reshape(1)
 
-    own, grad, other, low, high = front(core, assistant_mask[0], inputs, upstream, weight, chips, rows)
+    operands = (pltpu.with_memory_space_constraint(x, pltpu.HBM) for x in (assistant_mask[0], inputs, upstream, weight))
+    own, grad, other, low, high = front(core, *operands, chips, rows)
     partner = lax.ppermute(other, "dp", [(i, i ^ 1) for i in range(n)])
     low, high = (from_behind(half, "pipe", -1) for half in (low, high))
     term = terms(partner, own_terms(own, grad, chips * (rows + 1)))

time: 70.9 us -> 68.2 us (0.962)
  the two profiles are of different devices: /device:TPU:38 before, /device:TPU:14 now
where the time goes in v6:
time: 68.2 us; the launch traced here: 67.9 us
  blocking collectives  41.8 us (61%)
  Pallas kernels  11.7 us (17%)
  starting transfers between devices  11.5 us (17%)
  local copies, waits for them, and re-layouts  1.62 us (2%)
  between operations  1.38 us (2%)
    unnamed x1, blocking collectives  41.8 us
    pallas_call x1, Pallas kernels, front(): pl.pallas_call(functools.partial(front_kernel, chips, rows), out_shape=(p...  6.5 us
    ppermute x2, starting transfers between devices, from_behind(): return lax.ppermute(block, axis, route)  6.13 us
    unnamed x1, starting transfers between devices  3.46 us
    pallas_call x1, Pallas kernels, finish(): pl.pallas_call(finish_kernel, out_shape=(weight_out, jax.ShapeDtypeStruct...  2.34 us
    ppermute x1, starting transfers between devices, local(): partner = lax.ppermute(other, 'dp', [(i, i ^ 1) for i in range(n)])  1.92 us
    unnamed x4, local copies, waits for them, and re-layouts  1.62 us
    pallas_call x1, Pallas kernels, terms(): pl.pallas_call(term_kernel, out_shape=jax.ShapeDtypeStruct((rows, width),...  1.42 us
  transfers between devices with their start and end apart: 4, of which 0 were waited for; matrix products, arithmetic and copies ran while one was open for 64% of the time, Pallas kernels for 4%

profile of v6, /device:TPU:14, one launch (start us, length us, event | category | flops | bytes accessed | tf_op | source)
XLA Modules:
  0.0 67.9 jit_solution(6717218062461048359)
XLA Ops:
  0.6 6.5 %front.1 = (bf16[464,1152]{1,0:T(8,128)(2,1)S(1)}, bf16[464,1024]{1,0:T(8,128)(2,1)S(1)}, bf16[464,2176]{1,0:T(8,128)(2,1)S(1)}, bf16[448,1024]{1,0:T(8,128)(2,1)}, bf16[448,1024]{1,0:T(8,128)(2,1)}) custom-call(s32[1]{0:T(128)} %bitcast.core_ref, s32[4,8192]{1,0:T(4,128)} %bitcast.13, bf16[448,2048]{1,0:T(8,128)(2,1)} %bitcast.11, ...), custom_call_target="tpu_custom_call" | custom-call | flops 1879048192 | bytes 14680064 | tf_op jit(solution)/shard_map/front/pallas_call | solution.py:93
  7.1 1.9 %collective-permute-start = (bf16[464,2176]{1,0:T(8,128)(2,1)S(1)}, bf16[464,2176]{1,0:T(8,128)(2,1)S(1)}, u32[]{:S(2)}, u32[]{:S(2)}) collective-permute-start(bf16[464,2176]{1,0:T(8,128)(2,1)S(1)} %get-tuple-element.9), channel_id=1, source_target_pairs={{0,32},{32,0},{64,96},{96,64},{128,160},{160,128},{192,224},{224,1... | collective-permute-start | bytes 6057992 | tf_op jit(solution)/shard_map/ppermute | solution.py:226
  9.1 2.8 %collective-permute-start.1 = (bf16[448,1024]{1,0:T(8,128)(2,1)}, bf16[448,1024]{1,0:T(8,128)(2,1)S(1)}, u32[]{:S(2)}, u32[]{:S(2)}) collective-permute-start(bf16[448,1024]{1,0:T(8,128)(2,1)} %get-tuple-element.12), channel_id=1, source_target_pairs={{1,0},{2,1},{3,2},{5,4},{6,5},{7,6},{9,8},{10,9},{11,10},{13,12},{... | collective-permute-start | bytes 2752520 | tf_op jit(solution)/shard_map/ppermute | solution.py:21
  11.9 3.3 %collective-permute-start.2 = (bf16[448,1024]{1,0:T(8,128)(2,1)}, bf16[448,1024]{1,0:T(8,128)(2,1)}, u32[]{:S(2)}, u32[]{:S(2)}) collective-permute-start(bf16[448,1024]{1,0:T(8,128)(2,1)} %get-tuple-element.13), channel_id=1, source_target_pairs={{1,0},{2,1},{3,2},{5,4},{6,5},{7,6},{9,8},{10,9},{11,10},{13,12},{... | collective-permute-start | bytes 2752520 | tf_op jit(solution)/shard_map/ppermute | solution.py:21
  15.2 1.4 %own_terms.1.first_ref = f32[1044,1024]{1,0:T(8,128)S(1)} custom-call(bf16[464,1152]{1,0:T(8,128)(2,1)S(1)} %get-tuple-element.10.own_ref, bf16[464,1024]{1,0:T(8,128)(2,1)S(1)} %get-tuple-element.11.grad_ref), custom_call_target="tpu_custom_call" | custom-call | flops 992083968 | bytes 6291456 | tf_op jit(solution)/shard_map/own_terms/pallas_call | solution.py:131
  16.6 0.0 collective-permute-done.partner_ref
  16.6 1.4 %terms.1 = bf16[1044,1024]{1,0:T(8,128)(2,1)S(1)} custom-call(bf16[464,2176]{1,0:T(8,128)(2,1)S(1)} %collective-permute-done.partner_ref, f32[1044,1024]{1,0:T(8,128)S(1)} %own_terms.1.first_ref), custom_call_target="tpu_custom_call" | custom-call | flops 992083968 | bytes 8388608 | tf_op jit(solution)/shard_map/terms/pallas_call | solution.py:152
  18.0 41.8 %fusion = bf16[88,1024]{1,0:T(8,128)(2,1)S(1)} fusion(bf16[1044,1024]{1,0:T(8,128)(2,1)S(1)} %terms.1), kind=kCustom, calls=%all-reduce-scatter | all-reduce-scatter fusion | flops 1081345 | bytes 2322432
  59.8 3.5 %collective-permute-start.3 = (bf16[11,1024]{1,0:T(8,128)(2,1)S(1)}, bf16[11,1024]{1,0:T(8,128)(2,1)S(1)}, u32[]{:S(2)}, u32[]{:S(2)}) collective-permute-start(bf16[11,1024]{1,0:T(8,128)(2,1)S(1)} %slice), channel_id=1, source_target_pairs={{0,64},{64,128},{128,192},{192,256},{256,320},{320,384},{384,448},... | collective-permute-start | bytes 67592
  63.3 1.3 %dynamic-slice.4 = u32[1]{0:T(128)} dynamic-slice(u32[768]{0:T(1024)} %constant.16, u32[]{:S(6)} %partition-id.4), dynamic_slice_sizes={1} | dynamic-slice | bytes 12
  65.2 0.0 collective-permute-done.3
  65.2 0.3 concatenate
  65.5 0.1 constant_dynamic-slice_fusion.mine_ref
  65.6 0.0 collective-permute-done.1.low_ref
  65.6 0.0 collective-permute-done.2.high_ref
  65.6 2.3 %finish.1 = (f32[86,8,128]{2,1,0:T(8,128)}, bf16[448,2048]{1,0:T(8,128)(2,1)}) custom-call(bf16[87,1024]{1,0:T(8,128)(2,1)S(1)} %constant_dynamic-slice_fusion.mine_ref, bf16[448,1024]{1,0:T(8,128)(2,1)S(1)} %collective-permute-done.1.low_ref, bf16[448,1024]{1,0:T(8,128)(2,1)} %collective-permute-done.2.high_ref), custom_call_target="tpu_custom_call" | custom-call | tf_op jit(solution)/shard_map/finish/pallas_call | solution.py:198
  (1 shorter events, 0.0 us)
Async XLA Ops:
  7.1 9.5 %collective-permute-start = (bf16[464,2176]{1,0:T(8,128)(2,1)S(1)}, bf16[464,2176]{1,0:T(8,128)(2,1)S(1)}, u32[]{:S(2)}, u32[]{:S(2)}) collective-permute-start(bf16[464,2176]{1,0:T(8,128)(2,1)S(1)} %get-tuple-element.9), channel_id=1, source_target_pairs={{0,32},{32,0},{64,96},{96,64},{128,160},{160,128},{192,224},{224,1... | collective-permute-start | bytes 6057992 | tf_op jit(solution)/shard_map/ppermute | solution.py:226
  9.1 56.5 %collective-permute-start.1 = (bf16[448,1024]{1,0:T(8,128)(2,1)}, bf16[448,1024]{1,0:T(8,128)(2,1)S(1)}, u32[]{:S(2)}, u32[]{:S(2)}) collective-permute-start(bf16[448,1024]{1,0:T(8,128)(2,1)} %get-tuple-element.12), channel_id=1, source_target_pairs={{1,0},{2,1},{3,2},{5,4},{6,5},{7,6},{9,8},{10,9},{11,10},{13,12},{... | collective-permute-start | bytes 2752520 | tf_op jit(solution)/shard_map/ppermute | solution.py:21
  11.9 53.7 %collective-permute-start.2 = (bf16[448,1024]{1,0:T(8,128)(2,1)}, bf16[448,1024]{1,0:T(8,128)(2,1)}, u32[]{:S(2)}, u32[]{:S(2)}) collective-permute-start(bf16[448,1024]{1,0:T(8,128)(2,1)} %get-tuple-element.13), channel_id=1, source_target_pairs={{1,0},{2,1},{3,2},{5,4},{6,5},{7,6},{9,8},{10,9},{11,10},{13,12},{... | collective-permute-start | bytes 2752520 | tf_op jit(solution)/shard_map/ppermute | solution.py:21
  59.8 5.4 %collective-permute-start.3 = (bf16[11,1024]{1,0:T(8,128)(2,1)S(1)}, bf16[11,1024]{1,0:T(8,128)(2,1)S(1)}, u32[]{:S(2)}, u32[]{:S(2)}) collective-permute-start(bf16[11,1024]{1,0:T(8,128)(2,1)S(1)} %slice), channel_id=1, source_target_pairs={{0,64},{64,128},{128,192},{192,256},{256,320},{320,384},{384,448},... | collective-permute-start | bytes 67592

commit v7 on v6

v7 whole, which is shorter than its diff:
```python
import functools

import jax
import jax.numpy as jnp
from jax import lax
from jax.experimental import pallas as pl
from jax.experimental.pallas import tpu as pltpu
from jax.sharding import PartitionSpec as P

DIGITS = 6
EXTRA = 16
TILE = 256
PARTS = 4
VM = pl.BlockSpec(memory_space=pltpu.VMEM)
ANY = pl.BlockSpec(memory_space=pl.ANY)


def from_behind(block, axis, distance):
    devices = range(lax.axis_size(axis))
    route = [(i - distance, i) for i in devices if i - distance in devices]
    return lax.ppermute(block, axis, route)


def front_kernel(
    chips, rows, core_ref, mask_ref, normed_ref, grad_ref, weight_ref, own_ref, own_grad_ref, other_ref, total_ref,
    mask, normed, weight, made, arrived, left,
):
    tokens, width = normed.shape
    lanes, columns = own_ref.shape[1], grad_ref.shape[1]
    step, slab = tokens // PARTS, width // PARTS
    beside = other_ref.at[:, pl.ds(lanes, columns)]
    loads = [
        pltpu.make_async_copy(grad_ref, own_grad_ref.at[pl.ds(0, tokens)], arrived.at[0]),
        pltpu.make_async_copy(mask_ref, mask, arrived.at[1]),
    ]
    for i in range(PARTS):
        at = pl.ds(i * step, step)
        loads.append(pltpu.make_async_copy(weight_ref.at[pl.ds(i * slab, slab)], weight.at[i], arrived.at[2 * i + 2]))
        loads.append(pltpu.make_async_copy(normed_ref.at[at], normed.at[at], arrived.at[2 * i + 3]))
    loads.append(pltpu.make_async_copy(grad_ref, beside.at[pl.ds(0, tokens)], arrived.at[2 * PARTS + 2]))
    for load in loads:
        load.start()

    at = lax.broadcasted_iota(jnp.int32, (EXTRA, lanes), 1)
    first = lax.broadcasted_iota(jnp.int32, (EXTRA, lanes), 0) == 0
    marks = first & (at % (rows + 1) == rows) & (at < chips * (rows + 1))
    marks = jnp.where(marks, 1.0, 0.0).astype(jnp.bfloat16)
    own_ref[tokens:, :] = marks
    other_ref[tokens:, :lanes] = marks
    lane = lax.broadcasted_iota(jnp.int32, (EXTRA, columns), 1)
    row = lax.broadcasted_iota(jnp.int32, (EXTRA, columns), 0)
    loads[1].wait()
    count = jnp.sum(mask[...])
    digit = jnp.bitwise_and(jnp.right_shift(count, 3 * jnp.minimum(lane, DIGITS)), 7)
    digit = jnp.where((lane < DIGITS) & (row == 0), digit, 0).astype(jnp.float32).astype(jnp.bfloat16)
    own_grad_ref[tokens:, :] = digit
    other_ref[tokens:, lanes:] = digit
    even = core_ref[0] == 0
    loads[0].wait()

    stores = []
    for i in range(PARTS):
        loads[2 * i + 2].wait()
        loads[2 * i + 3].wait()
        made[i] = lax.dot_general(
            own_grad_ref[:tokens, :], weight[i], (((1,), (1,)), ((), ())), preferred_element_type=jnp.float32
        ).astype(jnp.bfloat16)
        packs = []
        for parity in range(2):
            pieces = []
            for j in range(chips):
                begin = (2 * j + parity) * rows
                end = min(begin + rows, width)
                pieces.append(normed[i * step : (i + 1) * step, begin:end])
                pieces.append(jnp.zeros((step, rows + 1 - (end - begin)), jnp.bfloat16))
            pieces.append(jnp.zeros((step, lanes - chips * (rows + 1)), jnp.bfloat16))
            packs.append(jnp.concatenate(pieces, axis=1))
        own_ref[i * step : (i + 1) * step, :] = jnp.where(even, packs[0], packs[1])
        other_ref[i * step : (i + 1) * step, :lanes] = jnp.where(even, packs[1], packs[0])
        stores.append(pltpu.make_async_copy(made.at[i], total_ref.at[:, pl.ds(i * slab, slab)], left.at[i]))
        stores[-1].start()
    loads[-1].wait()
    for store in stores:
        store.wait()


def front(core, mask, inputs, upstream, weight, chips, rows):
    lanes = -(-chips * (rows + 1) // 128) * 128
    (tokens, width), columns = inputs.shape, upstream.shape[1]
    height = tokens + EXTRA
    bf16 = jnp.bfloat16
    hbm = pl.BlockSpec(memory_space=pltpu.HBM)
    return pl.pallas_call(
        functools.partial(front_kernel, chips, rows),
        out_shape=(
            pltpu.VMEM((height, lanes), bf16),
            pltpu.VMEM((height, columns), bf16),
            pltpu.VMEM((height, lanes + columns), bf16),
            pltpu.HBM((tokens, width), bf16),
        ),
        in_specs=[pl.BlockSpec(memory_space=pltpu.SMEM)] + [hbm] * 4,
        out_specs=(VM, VM, VM, hbm),
        scratch_shapes=[
            pltpu.VMEM(mask.shape, mask.dtype),
            pltpu.VMEM(inputs.shape, bf16),
            pltpu.VMEM((PARTS, width // PARTS, columns), bf16),
            pltpu.VMEM((PARTS, tokens, width // PARTS), bf16),
            pltpu.SemaphoreType.DMA((2 * PARTS + 3,)),
            pltpu.SemaphoreType.DMA((PARTS,)),
        ],
        name="front",
        compiler_params=pltpu.CompilerParams(vmem_limit_bytes=40 << 20),
        cost_estimate=pl.CostEstimate(flops=2 * upstream.size * width, bytes_accessed=14 << 20, transcendentals=0),
    )(core, mask, inputs, upstream, weight)


def product(left, right):
    return lax.dot_general(left, right, (((0,), (0,)), ((), ())), preferred_element_type=jnp.float32)


def own_kernel(own_ref, grad_ref, out_ref):
    for m in range(0, out_ref.shape[0], TILE):
        size = min(TILE, out_ref.shape[0] - m)
        out_ref[m : m + size, :] = product(own_ref[:, m : m + size], grad_ref[...])


def own_terms(own, grad, rows):
    width = grad.shape[1]
    return pl.pallas_call(
        own_kernel,
        out_shape=jax.ShapeDtypeStruct((rows, width), jnp.float32),
        in_specs=[VM] * 2,
        out_specs=VM,
        name="own_terms",
        compiler_params=pltpu.CompilerParams(vmem_limit_bytes=20 << 20),
        cost_estimate=pl.CostEstimate(flops=2 * own.shape[0] * rows * width, bytes_accessed=6 << 20, transcendentals=0),
    )(own, grad)


def term_kernel(partner_ref, first_ref, out_ref):
    lanes = partner_ref.shape[1] - out_ref.shape[1]
    for m in range(0, out_ref.shape[0], TILE):
        size = min(TILE, out_ref.shape[0] - m)
        tile = product(partner_ref[:, m : m + size], partner_ref[:, lanes:]) + first_ref[m : m + size, :]
        out_ref[m : m + size, :] = tile.astype(out_ref.dtype)


def terms(partner, first):
    rows, width = first.shape
    return pl.pallas_call(
        term_kernel,
        out_shape=jax.ShapeDtypeStruct((rows, width), jnp.bfloat16),
        in_specs=[VM] * 2,
        out_specs=VM,
        name="terms",
        compiler_params=pltpu.CompilerParams(vmem_limit_bytes=20 << 20),
        cost_estimate=pl.CostEstimate(
            flops=2 * partner.shape[0] * rows * width, bytes_accessed=8 << 20, transcendentals=0
        ),
    )(partner, first)


def finish_kernel(mine_ref, passed_ref, weight_out_ref, passed_out_ref, mine, passed, weight_out, arrived, left):
    rows = weight_out_ref.shape[0]
    parts = PARTS
    step = passed.shape[0] // parts
    loads = [pltpu.make_async_copy(mine_ref, mine, arrived.at[parts])]
    for i in range(parts):
        at = pl.ds(i * step, step)
        loads.append(pltpu.make_async_copy(passed_ref.at[at], passed.at[at], arrived.at[i]))
    for load in loads:
        load.start()
    loads[0].wait()
    digits = mine[rows : rows + 1, :128].astype(jnp.float32)
    lane = lax.broadcasted_iota(jnp.int32, (1, 128), 1)
    scale = jnp.where(lane < DIGITS, jnp.left_shift(1, 3 * jnp.minimum(lane, DIGITS)), 0).astype(jnp.float32)
    inverse = 1.0 / jnp.sum(digits * scale)
    for q in range(weight_out_ref.shape[1]):
        weight_out[:, q, :] = mine[:rows, 128 * q : 128 * (q + 1)].astype(jnp.float32) * inverse
    stores = [pltpu.make_async_copy(weight_out, weight_out_ref, left.at[parts])]
    stores[0].start()
    for i in range(parts):
        at = pl.ds(i * step, step)
        loads[i + 1].wait()
        passed[at, :] = (passed[at, :].astype(jnp.float32) * inverse).astype(jnp.bfloat16)
        stores.append(pltpu.make_async_copy(passed.at[at], passed_out_ref.at[at], left.at[i]))
        stores[-1].start()
    for store in stores:
        store.wait()


def finish(mine, passed):
    weight_out = jax.ShapeDtypeStruct((mine.shape[0] - 1, mine.shape[1] // 128, 128), jnp.float32)
    return pl.pallas_call(
        finish_kernel,
        out_shape=(weight_out, jax.ShapeDtypeStruct(passed.shape, jnp.bfloat16)),
        in_specs=[ANY, ANY],
        out_specs=(ANY, ANY),
        scratch_shapes=[
            pltpu.VMEM(mine.shape, mine.dtype),
            pltpu.VMEM(passed.shape, passed.dtype),
            pltpu.VMEM(weight_out.shape, weight_out.dtype),
            pltpu.SemaphoreType.DMA((PARTS + 1,)),
            pltpu.SemaphoreType.DMA((PARTS + 1,)),
        ],
        name="finish",
        compiler_params=pltpu.CompilerParams(vmem_limit_bytes=20 << 20),
    )(mine, passed)


def local(normed, w_value, grad_value, assistant_mask):
    inputs = normed[0]
    weight = w_value[0]
    upstream = grad_value[0]
    n = lax.axis_size("dp")
    chips = n // 2
    rows = -(-inputs.shape[1] // n)
    core = lax.rem(lax.axis_index("dp"), 2).reshape(1)

    operands = (pltpu.with_memory_space_constraint(x, pltpu.HBM) for x in (assistant_mask[0], inputs, upstream, weight))
    own, grad, other, total = front(core, *operands, chips, rows)
    partner = lax.ppermute(other, "dp", [(i, i ^ 1) for i in range(n)])
    passed = from_behind(total, "pipe", -1)
    term = terms(partner, own_terms(own, grad, chips * (rows + 1)))
    parity = [[2 * z + c for z in range(chips)] for c in range(2)]
    mine = lax.psum_scatter(term, "dp", scatter_dimension=0, tiled=True, axis_index_groups=parity)
    weight_grad, input_grad = finish(mine, passed)
    return (weight_grad.reshape(1, 1, rows, -1), input_grad[None])


def solution(mesh):
    return jax.shard_map(
        local,
        mesh=mesh,
        in_specs=(
            P("pipe", "dp", "tensor"),
            P("pipe", "tensor", None),
            P("pipe", "dp", None),
            P("dp", None, None),
        ),
        out_specs=(P("pipe", "tensor", "dp", None), P("pipe", "dp", "tensor")),
        check_vma=False,
    )
```

time: 68.2 us -> 65.2 us (0.956)
  the two profiles are of different devices: /device:TPU:14 before, /device:TPU:1 now
where the time goes in v7:
time: 65.2 us; the launch traced here: 64.9 us
  blocking collectives  30.1 us (46%)
  starting transfers between devices  15.9 us (24%)
  Pallas kernels  10.9 us (17%)
  waiting for transfers between devices  5.09 us (8%)
  local copies, waits for them, and re-layouts  1.62 us (2%)
  between operations  1.37 us (2%)
    unnamed x1, blocking collectives  30.1 us
    ppermute x1, starting transfers between devices, local(): partner = lax.ppermute(other, 'dp', [(i, i ^ 1) for i in range(n)])  12.4 us
    pallas_call x1, Pallas kernels, front(): pl.pallas_call(functools.partial(front_kernel, chips, rows), out_shape=(p...  5.41 us
    ppermute x1, waiting for transfers between devices, from_behind(): return lax.ppermute(block, axis, route)  4.14 us
    pallas_call x1, Pallas kernels, finish(): pl.pallas_call(finish_kernel, out_shape=(weight_out, jax.ShapeDtypeStruct...  2.69 us
    unnamed x1, starting transfers between devices  2.18 us
    unnamed x4, local copies, waits for them, and re-layouts  1.62 us
    pallas_call x1, Pallas kernels, terms(): pl.pallas_call(term_kernel, out_shape=jax.ShapeDtypeStruct((rows, width),...  1.4 us
  transfers between devices with their start and end apart: 3, of which 2 were waited for; matrix products, arithmetic and copies ran while one was open for 49% of the time, Pallas kernels for 4%

profile of v7, /device:TPU:1, one launch (start us, length us, event | category | flops | bytes accessed | tf_op | source)
XLA Modules:
  0.0 64.9 jit_solution(10267138849440895294)
XLA Ops:
  0.6 5.4 %front.1 = (bf16[464,1152]{1,0:T(8,128)(2,1)S(1)}, bf16[464,1024]{1,0:T(8,128)(2,1)S(1)}, bf16[464,2176]{1,0:T(8,128)(2,1)S(1)}, bf16[448,2048]{1,0:T(8,128)(2,1)}) custom-call(s32[1]{0:T(128)} %bitcast.core_ref, s32[4,8192]{1,0:T(4,128)} %bitcast.13, bf16[448,2048]{1,0:T(8,128)(2,1)} %bitcast.11, bf16[448,1024]{1,0:T(8,128)(2,1)} %bitcast.12, ...), custom_call_target="tpu_custom_call" | custom-call | flops 1879048192 | bytes 14680064 | tf_op jit(solution)/shard_map/front/pallas_call | solution.py:93
  6.1 12.4 %collective-permute-start = (bf16[464,2176]{1,0:T(8,128)(2,1)S(1)}, bf16[464,2176]{1,0:T(8,128)(2,1)S(1)}, u32[]{:S(2)}, u32[]{:S(2)}) collective-permute-start(bf16[464,2176]{1,0:T(8,128)(2,1)S(1)} %get-tuple-element.8), channel_id=1, source_target_pairs={{0,32},{32,0},{64,96},{96,64},{128,160},{160,128},{192,224},{224,1... | collective-permute-start | bytes 6057992 | tf_op jit(solution)/shard_map/ppermute | solution.py:222
  18.5 1.3 %collective-permute-start.1 = (bf16[448,2048]{1,0:T(8,128)(2,1)}, bf16[448,2048]{1,0:T(8,128)(2,1)}, u32[]{:S(2)}, u32[]{:S(2)}) collective-permute-start(bf16[448,2048]{1,0:T(8,128)(2,1)} %get-tuple-element.11), channel_id=1, source_target_pairs={{1,0},{2,1},{3,2},{5,4},{6,5},{7,6},{9,8},{10,9},{11,10},{13,12},{... | collective-permute-start | bytes 5505032 | tf_op jit(solution)/shard_map/ppermute | solution.py:21
  19.8 1.4 %own_terms.1.first_ref = f32[1044,1024]{1,0:T(8,128)S(1)} custom-call(bf16[464,1152]{1,0:T(8,128)(2,1)S(1)} %get-tuple-element.9.own_ref, bf16[464,1024]{1,0:T(8,128)(2,1)S(1)} %get-tuple-element.10.grad_ref), custom_call_target="tpu_custom_call" | custom-call | flops 992083968 | bytes 6291456 | tf_op jit(solution)/shard_map/own_terms/pallas_call | solution.py:129
  21.2 1.0 %collective-permute-done.partner_ref = bf16[464,2176]{1,0:T(8,128)(2,1)S(1)} collective-permute-done((bf16[464,2176]{1,0:T(8,128)(2,1)S(1)}, bf16[464,2176]{1,0:T(8,128)(2,1)S(1)}, u32[]{:S(2)}, u32[]{:S(2)}) %collective-permute-start) | collective-permute-done | bytes 2019360 | tf_op jit(solution)/shard_map/ppermute | solution.py:222
  22.1 1.4 %terms.1 = bf16[1044,1024]{1,0:T(8,128)(2,1)S(1)} custom-call(bf16[464,2176]{1,0:T(8,128)(2,1)S(1)} %collective-permute-done.partner_ref, f32[1044,1024]{1,0:T(8,128)S(1)} %own_terms.1.first_ref), custom_call_target="tpu_custom_call" | custom-call | flops 992083968 | bytes 8388608 | tf_op jit(solution)/shard_map/terms/pallas_call | solution.py:150
  23.5 30.1 %fusion = bf16[88,1024]{1,0:T(8,128)(2,1)S(1)} fusion(bf16[1044,1024]{1,0:T(8,128)(2,1)S(1)} %terms.1), kind=kCustom, calls=%all-reduce-scatter | all-reduce-scatter fusion | flops 1081345 | bytes 2322432
  53.6 2.2 %collective-permute-start.2 = (bf16[11,1024]{1,0:T(8,128)(2,1)S(1)}, bf16[11,1024]{1,0:T(8,128)(2,1)S(1)}, u32[]{:S(2)}, u32[]{:S(2)}) collective-permute-start(bf16[11,1024]{1,0:T(8,128)(2,1)S(1)} %slice), channel_id=1, source_target_pairs={{0,64},{64,128},{128,192},{192,256},{256,320},{320,384},{384,448},... | collective-permute-start | bytes 67592
  55.8 1.3 %dynamic-slice.4 = u32[1]{0:T(128)} dynamic-slice(u32[768]{0:T(1024)} %constant.16, u32[]{:S(6)} %partition-id.4), dynamic_slice_sizes={1} | dynamic-slice | bytes 12
  57.7 0.0 collective-permute-done.2
  57.7 0.3 concatenate
  58.0 0.1 constant_dynamic-slice_fusion.mine_ref
  58.1 4.1 %collective-permute-done.1.passed_ref = bf16[448,2048]{1,0:T(8,128)(2,1)} collective-permute-done((bf16[448,2048]{1,0:T(8,128)(2,1)}, bf16[448,2048]{1,0:T(8,128)(2,1)}, u32[]{:S(2)}, u32[]{:S(2)}) %collective-permute-start.1) | collective-permute-done | bytes 1835040 | tf_op jit(solution)/shard_map/ppermute | solution.py:21
  62.2 2.7 %finish.1 = (f32[86,8,128]{2,1,0:T(8,128)}, bf16[448,2048]{1,0:T(8,128)(2,1)}) custom-call(bf16[87,1024]{1,0:T(8,128)(2,1)S(1)} %constant_dynamic-slice_fusion.mine_ref, bf16[448,2048]{1,0:T(8,128)(2,1)} %collective-permute-done.1.passed_ref), custom_call_target="tpu_custom_call" | custom-call | tf_op jit(solution)/shard_map/finish/pallas_call | solution.py:194
  (1 shorter events, 0.0 us)
Async XLA Ops:
  6.1 16.0 %collective-permute-start = (bf16[464,2176]{1,0:T(8,128)(2,1)S(1)}, bf16[464,2176]{1,0:T(8,128)(2,1)S(1)}, u32[]{:S(2)}, u32[]{:S(2)}) collective-permute-start(bf16[464,2176]{1,0:T(8,128)(2,1)S(1)} %get-tuple-element.8), channel_id=1, source_target_pairs={{0,32},{32,0},{64,96},{96,64},{128,160},{160,128},{192,224},{224,1... | collective-permute-start | bytes 6057992 | tf_op jit(solution)/shard_map/ppermute | solution.py:222
  18.5 43.8 %collective-permute-start.1 = (bf16[448,2048]{1,0:T(8,128)(2,1)}, bf16[448,2048]{1,0:T(8,128)(2,1)}, u32[]{:S(2)}, u32[]{:S(2)}) collective-permute-start(bf16[448,2048]{1,0:T(8,128)(2,1)} %get-tuple-element.11), channel_id=1, source_target_pairs={{1,0},{2,1},{3,2},{5,4},{6,5},{7,6},{9,8},{10,9},{11,10},{13,12},{... | collective-permute-start | bytes 5505032 | tf_op jit(solution)/shard_map/ppermute | solution.py:21
  53.6 4.1 %collective-permute-start.2 = (bf16[11,1024]{1,0:T(8,128)(2,1)S(1)}, bf16[11,1024]{1,0:T(8,128)(2,1)S(1)}, u32[]{:S(2)}, u32[]{:S(2)}) collective-permute-start(bf16[11,1024]{1,0:T(8,128)(2,1)S(1)} %slice), channel_id=1, source_target_pairs={{0,64},{64,128},{128,192},{192,256},{256,320},{320,384},{384,448},... | collective-permute-start | bytes 67592
